TPU v7x, 32 devices: a whole 2x2x4 slice. The times are simulated.
32 devices in a mesh: sec: 4 (over y, x), gx: 8 (over z, core).
Axes of the slice: x: 2, y: 2, z: 4, core: 2. Of those that a mesh axis runs over, the one named last changes fastest.
Arguments:
- pressure_start: float32 [16, 128, 1024], P('sec', 'gx'), may hold values from -8 to 8
- soil_type: int32 [16, 128, 1024], P('sec', 'gx'), may hold values from 0 to 11
- saturated_conductivity: float32 [12], replicated, may hold values from 0.2 to 5
- storage_coefficient: float32 [12], replicated, may hold values from 0.1 to 1
- rainfall: float32 [3, 128, 1024], P(None, 'gx'), may hold values from 0 to 2
Outputs:
- pressure: float32 [16, 128, 1024], P('sec', 'gx')
- inflow: float32 [4, 3, 128, 1024], P('sec', None, 'gx')
All inputs are finite; a program needn't handle non-finite values.
Results may differ from a plain program's by a relative error of at most 0.0001.
Values sent between devices are 32-bit elements; how exact they have to be, the bound alone decides.
A program may use at most 64 MiB of HBM per device.

v0:
```python
import functools

import jax
import jax.numpy as jnp
from jax import lax
from jax.experimental import pallas as pl
from jax.experimental.pallas import tpu as pltpu
from jax.sharding import PartitionSpec as P


MESH = pl.DeviceIdType.MESH
RIM = 8
LANES = 128
ITERS = 4


def place_of(s):
    return s + s // 2 - 2 * (s // 3)


def coefficients(g, h):
    nu = [g[0], h[0]]
    for k in range(1, ITERS):
        nu.append(2.0 * g[k] - nu[0])
        nu.append(4.0 * h[k] - 2.0 * nu[1] - nu[2 * k - 1])

    def gram(i, j):
        return 0.5 * (nu[i + j] + nu[abs(i - j)])

    def gram_a(i, j):
        shifted = gram(i, 1) if j == 0 else 0.5 * (gram(i, j + 1) + gram(i, j - 1))
        return gram(i, j) - shifted

    G = [[gram(i, j) for j in range(ITERS)] for i in range(ITERS)]
    H = [[gram_a(max(i, j), min(i, j)) for j in range(ITERS)] for i in range(ITERS)]
    zero = jnp.zeros_like(g[0])

    def form(matrix, v, top):
        total = zero
        for i in range(top + 1):
            row = matrix[i][i] * v[i]
            for j in range(i):
                row = row + 2.0 * matrix[i][j] * v[j]
            total = total + row * v[i]
        return total

    z = [zero + 1.0] + [zero] * (ITERS - 1)
    p = list(z)
    x = [zero] * ITERS
    rz = nu[0]
    for k in range(ITERS):
        curve = form(H, p, k)
        alpha = jnp.where(curve > 0.0, rz / jnp.where(curve > 0.0, curve, 1.0), 0.0)
        x = [a + alpha * b for a, b in zip(x, p)]
        if k + 1 < ITERS:
            image = list(p)
            for i in range(k + 1):
                if i == 0:
                    image[1] = image[1] - p[0]
                else:
                    image[i + 1] = image[i + 1] - 0.5 * p[i]
                    image[i - 1] = image[i - 1] - 0.5 * p[i]
            z = [a - alpha * b for a, b in zip(z, image)]
            new = jnp.maximum(form(G, z, k + 1), 0.0)
            beta = jnp.where(rz > 0.0, new / jnp.where(rz > 0.0, rz, 1.0), 0.0)
            p = [a + beta * b for a, b in zip(z, p)]
            rz = new
    return x


def kernel(
    n_sec, n_gx, steps, kinds,
    start_ref, soil_ref, cond_ref, store_ref, rain_ref,
    out_ref, flow_ref,
    head, soils, kind, store, cond, cap, face_l, face_r, face_c, diag, dinv, t0, t1, t2, t3,
    water, enter, leave, rainx, flows, pack_out, pack_in, soil_out, soil_in, landed, stats,
    met_sem, own_sem, swap_send, swap_recv, col_send, col_recv, row_send, row_recv, land_send, land_recv,
    sum_send, sum_recv, flow_send, flow_recv, back_send, back_recv,
):
    f32 = jnp.float32
    layers, rows, wide = start_ref.shape
    cols = wide // n_sec
    total = layers * n_sec
    sec, gx = lax.axis_index("sec"), lax.axis_index("gx")
    here = place_of(sec)
    ext_r, ext_c = rows + 2 * RIM, cols + LANES
    own = (slice(0, rows), slice(0, cols))

    def at(place):
        return pl.ds(pl.multiple_of(place * cols, LANES), cols)

    def layers_of(s):
        return pl.ds(1 + s * layers, layers)

    sec_peers = [lax.rem(sec + k, n_sec) for k in range(1, n_sec)]
    gx_peers = [lax.rem(gx + k, n_gx) for k in range(1, n_gx)]
    everyone = [
        {"sec": lax.rem(sec + i, n_sec), "gx": lax.rem(gx + j, n_gx)}
        for j in range(n_gx) for i in range(n_sec) if i + j
    ]
    barrier = pltpu.get_barrier_semaphore()
    for peer in sec_peers:
        pl.semaphore_signal(barrier, inc=1, device_id={"sec": peer}, device_id_type=MESH)
    for peer in gx_peers:
        pl.semaphore_signal(barrier, inc=1, device_id={"gx": peer}, device_id_type=MESH)

    plane = jnp.zeros((ext_r, ext_c), f32)
    for ref in (head, cond, t0, t1, t2, t3, face_l):
        ref[0] = plane
        ref[total + 1] = plane
    for d in (0, 1):
        rim = slice(rows + d * RIM, rows + d * RIM + RIM)

        @pl.when(gx == n_gx - 1 if d == 0 else gx == 0)
        def _(d=d, rim=rim):
            def wipe(l, carry):
                head[l + 1, rim, :] = jnp.zeros((RIM, ext_c), f32)
                soils[l + 1, rim, :] = jnp.zeros((RIM, ext_c), jnp.int32)
                for c in range(steps - 1):
                    for k in range(ITERS):
                        landed[c, k, d, l] = jnp.zeros((RIM, cols), f32)
                return carry

            lax.fori_loop(0, total, wipe, 0)
            for c in range(steps):
                rainx[c, rim, :] = jnp.zeros((RIM, ext_c), f32)

        @pl.when(here == n_sec - 1 if d == 0 else here == 0)
        def _(d=d):
            for c in range(steps):
                pack_in[c, d] = jnp.zeros((ext_r, LANES), f32)
            soil_in[d] = jnp.zeros((ext_r, LANES), jnp.int32)

    at_row = lax.broadcasted_iota(jnp.int32, (ext_r, ext_c), 0)
    at_col = lax.broadcasted_iota(jnp.int32, (ext_r, ext_c), 1)
    outside = (at_col >= cols + RIM) & (at_col < ext_c - RIM)
    outside = outside | ((at_row >= rows) & (at_row < rows + RIM) & (gx == n_gx - 1))
    outside = outside | ((at_row >= rows + RIM) & (gx == 0))
    outside = outside | ((at_col >= cols) & (at_col < cols + RIM) & (here == n_sec - 1))
    outside = outside | ((at_col >= ext_c - RIM) & (here == 0))

    lane = lax.broadcasted_iota(jnp.int32, (ext_r, LANES), 1)
    after = pl.multiple_of(lax.rem(here + 1, n_sec) * cols, LANES)
    before = pl.multiple_of(lax.rem(here + n_sec - 1, n_sec) * cols + cols - LANES, LANES)
    for c in range(steps):
        rainx[c, 0:rows, 0:cols] = rain_ref[c, :, at(here)]
        rainx[c, 0:rows, cols:] = jnp.where(
            lane[0:rows] < LANES // 2, rain_ref[c, :, pl.ds(after, LANES)], rain_ref[c, :, pl.ds(before, LANES)]
        )
    pl.semaphore_wait(barrier, n_sec + n_gx - 2)
    for peer in sec_peers:
        pl.semaphore_signal(met_sem, inc=1, device_id={"sec": peer}, device_id_type=MESH)

    swaps = []
    for f, (src, dst) in enumerate(((start_ref, head), (soil_ref, soils))):
        moves = []
        swaps.append(moves)
        copy = pltpu.make_async_copy(
            src.at[:, :, at(here)], dst.at[layers_of(sec), 0:rows, 0:cols], own_sem.at[f]
        )
        copy.start()
        moves.append(copy)
        for k, peer in enumerate(sec_peers):
            copy = pltpu.make_async_remote_copy(
                src_ref=src.at[:, :, at(place_of(peer))],
                dst_ref=dst.at[layers_of(sec), 0:rows, 0:cols],
                send_sem=swap_send.at[f, k],
                recv_sem=swap_recv.at[f, k],
                device_id={"sec": peer},
                device_id_type=MESH,
            )
            copy.start()
            moves.append(copy)

    def packed(field, low):
        outs = jnp.zeros((ext_r, LANES), field.dtype)
        for l in range(total):
            if low:
                tile = field[1 + l, :, 0:LANES]
                shift = RIM * l
            else:
                tile = field[1 + l, :, cols - LANES:cols]
                shift = (RIM * l + RIM) % LANES
            moved = pltpu.roll(tile, shift, 1) if shift else tile
            outs = jnp.where(lane // RIM == l, moved, outs)
        return outs

    def send_cols(slot, field):
        out, _ = packs(slot)
        out[0] = packed(field, True)
        out[1] = packed(field, False)
        for d in (0, 1):
            @pl.when(here > 0 if d == 0 else here < n_sec - 1)
            def _(d=d):
                col_copy(slot, d).start()

    def packs(slot):
        return (pack_out.at[slot], pack_in.at[slot]) if slot < steps else (soil_out, soil_in)

    def col_copy(slot, d):
        return pltpu.make_async_remote_copy(
            src_ref=packs(slot)[0].at[d],
            dst_ref=packs(slot)[1].at[d],
            send_sem=col_send.at[slot, d],
            recv_sem=col_recv.at[slot, d],
            device_id={"sec": place_of(lax.rem(here + n_sec - 1, n_sec) if d == 0 else lax.rem(here + 1, n_sec))},
            device_id_type=MESH,
        )

    def take_cols(slot, field):
        @pl.when(here > 0)
        def _():
            col_copy(slot, 0).wait_send()
            col_copy(slot, 1).wait_recv()

        @pl.when(here < n_sec - 1)
        def _():
            col_copy(slot, 1).wait_send()
            col_copy(slot, 0).wait_recv()

        taken = packs(slot)[1]
        right, left, nil = taken[0], taken[1], jnp.zeros((ext_r, LANES), field.dtype)
        for l in range(total):
            a, b = (-RIM * l) % LANES, (LANES - RIM - RIM * l) % LANES
            ra = pltpu.roll(right, a, 1) if a else right
            rb = pltpu.roll(left, b, 1) if b else left
            field[1 + l, :, cols:] = jnp.where(lane < RIM, ra, jnp.where(lane >= LANES - RIM, rb, nil))

    def row_copy(slot, field, first, count, width, d):
        src = pl.ds(0, RIM) if d == 0 else pl.ds(rows - RIM, RIM)
        dst = pl.ds(rows, RIM) if d == 0 else pl.ds(rows + RIM, RIM)
        return pltpu.make_async_remote_copy(
            src_ref=field.at[pl.ds(first, count), src, 0:width],
            dst_ref=field.at[pl.ds(first, count), dst, 0:width],
            send_sem=row_send.at[slot, d],
            recv_sem=row_recv.at[slot, d],
            device_id={"gx": lax.rem(gx + n_gx - 1, n_gx) if d == 0 else lax.rem(gx + 1, n_gx)},
            device_id_type=MESH,
        )

    def send_rows(*what):
        for d in (0, 1):
            @pl.when(gx > 0 if d == 0 else gx < n_gx - 1)
            def _(d=d):
                row_copy(*what, d).start()

    def take_rows(*what):
        @pl.when(gx > 0)
        def _():
            row_copy(*what, 0).wait_send()
            row_copy(*what, 1).wait_recv()

        @pl.when(gx < n_gx - 1)
        def _():
            row_copy(*what, 1).wait_send()
            row_copy(*what, 0).wait_recv()

    def shift(v, by, axis):
        return pltpu.roll(v, by % v.shape[axis], axis)

    def harmonic(a, b):
        return 2.0 * a * b / jnp.maximum(a + b, 1e-30)

    def folded(v):
        out = None
        for i in range(0, rows, RIM):
            for j in range(0, cols, LANES):
                part = v[i:i + RIM, j:j + LANES]
                out = part if out is None else out + part
        return out

    none = jnp.zeros((RIM, LANES), f32)
    basis = (t0, t1, t2, t3)

    def back_copy(k, peer):
        return pltpu.make_async_remote_copy(
            src_ref=head.at[layers_of(peer), 0:rows, 0:cols],
            dst_ref=out_ref.at[:, :, at(here)],
            send_sem=back_send.at[k],
            recv_sem=back_recv.at[k],
            device_id={"sec": peer},
            device_id_type=MESH,
        )

    outgoing = []
    for c in range(steps):
        if c == 0:
            fields = ((0, head, 1, total, cols), (1, soils, 1, total, cols), (2, rainx, 0, steps, ext_c))
            for f in range(2):
                for copy in swaps[f]:
                    copy.wait()
                send_rows(*fields[f])
            send_rows(*fields[2])
            take_rows(*fields[0])
            send_cols(c, head)
            take_rows(*fields[1])
            send_cols(steps, soils)
            take_rows(*fields[2])

            spot = lax.broadcasted_iota(jnp.int32, (ext_r, LANES), 1)
            of_cond = jnp.zeros((ext_r, LANES), f32)
            of_store = jnp.zeros((ext_r, LANES), f32)
            for k in range(kinds):
                of_cond = jnp.where(spot == k, cond_ref[k], of_cond)
                of_store = jnp.where(spot == k, store_ref[k], of_store)

            def look(lanes, l, carry):
                for j in range(lanes.start, lanes.stop, LANES):
                    which = soils[l, :, j:j + LANES]
                    hide = outside[:, j:j + LANES]
                    a = jnp.take_along_axis(of_cond, which, axis=1, mode="promise_in_bounds")
                    b = jnp.take_along_axis(of_store, which, axis=1, mode="promise_in_bounds")
                    kind[l, :, j:j + LANES] = jnp.where(hide, 0.0, a)
                    store[l, :, j:j + LANES] = jnp.where(hide, 0.0, b)
                return carry

        else:
            send_cols(c, head)

        def soil(lanes, s, carry):
            amount = jnp.zeros((ext_r, lanes.stop - lanes.start), f32)
            for j in range(layers):
                l = 1 + s * layers + j
                sat = jax.nn.sigmoid(head[l, :, lanes])
                cond[l, :, lanes] = kind[l, :, lanes] * (0.05 + sat * sat)
                cap[l, :, lanes] = store[l, :, lanes] * (0.1 + sat * (1.0 - sat))
                amount = amount + sat
            water[s, :, lanes] = amount
            return carry

        def couple(lanes):
            depth = jnp.float32(layers)
            below = jnp.zeros((ext_r, lanes.stop - lanes.start), f32)
            slopes = [None] * n_sec
            for s in reversed(range(n_sec)):
                amount = water[s, :, lanes]
                slopes[s] = amount / depth * (0.5 + 0.5 * below / (below + depth))
                below = below + amount
            entering = rainx[c, :, lanes]
            for s in range(n_sec):
                enter[s, :, lanes] = entering
                if lanes.start == 0:
                    flows[s, c] = entering[own]
                entering = slopes[s] * entering + 0.5 * cond[(s + 1) * layers, :, lanes]
                leave[s, :, lanes] = entering

        def faces(lanes, l, carry):
            k = cond[l, :, lanes]
            face_l[l, :, lanes] = harmonic(k, cond[l + 1, :, lanes])
            face_r[l, :, lanes] = harmonic(k, shift(k, -1, 0))
            return carry

        def faces_across(l, carry):
            k = cond[l]
            face_c[l] = harmonic(k, shift(k, -1, 1))
            return carry

        def prepare(lanes):
            if c == 0:
                lax.fori_loop(1, total + 1, functools.partial(look, lanes), 0)
            lax.fori_loop(0, n_sec, functools.partial(soil, lanes), 0)
            couple(lanes)
            lax.fori_loop(1, total + 1, functools.partial(faces, lanes), 0)

        prepare(slice(0, cols))
        own_flow = pltpu.make_async_copy(flows.at[sec, c], flow_ref.at[0, c, :, at(here)], own_sem.at[3 + c])
        own_flow.start()
        late = [own_flow]
        for k, peer in enumerate(sec_peers):
            copy = pltpu.make_async_remote_copy(
                src_ref=flows.at[peer, c],
                dst_ref=flow_ref.at[0, c, :, at(here)],
                send_sem=flow_send.at[c, k],
                recv_sem=flow_recv.at[c, k],
                device_id={"sec": peer},
                device_id_type=MESH,
            )
            copy.start()
            late.append(copy)
        outgoing += late

        if c == 0:
            take_cols(steps, soils)
        take_cols(c, head)
        prepare(slice(cols, ext_c))
        lax.fori_loop(1, total + 1, faces_across, 0)

        def first(s, acc):
            for j in range(layers):
                l = 1 + s * layers + j
                up, down = face_l[l - 1], face_l[l]
                fr, fc = face_r[l], face_c[l]
                v = head[l]
                whole = cap[l] + up + down + fr + shift(fr, 1, 0) + fc + shift(fc, 1, 1)
                flux_r = fr * (shift(v, -1, 0) - v)
                flux_c = fc * (shift(v, -1, 1) - v)
                res = up - down + up * (head[l - 1] - v) + down * (head[l + 1] - v)
                res = res + flux_r - shift(flux_r, 1, 0) + flux_c - shift(flux_c, 1, 1)
                if j == 0:
                    res = res + enter[s]
                if j == layers - 1:
                    res = res - leave[s]
                inverse = jnp.where(whole > 0.0, 1.0 / jnp.maximum(whole, 1e-30), 0.0)
                z = res * inverse
                diag[l] = whole
                dinv[l] = inverse
                t0[l] = z
                acc = acc + folded(res * z)
            return acc

        def land_copy(k, d, c=c):
            src = pl.ds(0, RIM) if d == 0 else pl.ds(rows - RIM, RIM)
            return pltpu.make_async_remote_copy(
                src_ref=basis[k].at[pl.ds(1, total), src, 0:cols],
                dst_ref=landed.at[c, k, d],
                send_sem=land_send.at[c, k, d],
                recv_sem=land_recv.at[c, k, d],
                device_id={"gx": lax.rem(gx + n_gx - 1, n_gx) if d == 0 else lax.rem(gx + 1, n_gx)},
                device_id_type=MESH,
            )

        def send_land(k):
            if c + 1 < steps:
                for d in (0, 1):
                    @pl.when(gx > 0 if d == 0 else gx < n_gx - 1)
                    def _(d=d):
                        land_copy(k, d).start()

        g = [lax.fori_loop(0, n_sec, first, none)]
        send_land(0)
        h = []
        for k in range(ITERS):
            def apply(l, acc, k=k):
                t = basis[k]
                fr, fc = face_r[l], face_c[l]
                v = t[l]
                near = face_l[l - 1] * t[l - 1] + face_l[l] * t[l + 1]
                near = near + fr * shift(v, -1, 0) + shift(fr * v, 1, 0)
                near = near + fc * shift(v, -1, 1) + shift(fc * v, 1, 1)
                ah = acc[0] + folded(v * near)
                ag = acc[1]
                if k + 1 < ITERS:
                    new = dinv[l] * near
                    if k > 0:
                        new = 2.0 * new - basis[k - 1][l]
                    basis[k + 1][l] = new
                    ag = ag + folded(diag[l] * new * new)
                return (ah, ag)

            ah, ag = lax.fori_loop(1, total + 1, apply, (none, none))
            h.append(ah)
            if k + 1 < ITERS:
                g.append(ag)
                send_land(k + 1)

        flat = jnp.concatenate([jnp.sum(v, axis=0, keepdims=True) for v in g + h], axis=0)
        part = LANES // (2 * ITERS)
        by = LANES // 2
        while by >= part:
            flat = flat + pltpu.roll(flat, by, 1)
            by //= 2
        which = lax.broadcasted_iota(jnp.int32, flat.shape, 0)
        group = lax.broadcasted_iota(jnp.int32, flat.shape, 1) // part
        mine = sec * n_gx + gx
        stats[c, mine] = jnp.sum(jnp.where(which == group, flat, 0.0), axis=0, keepdims=True)
        if c == 0:
            pl.semaphore_wait(met_sem, n_sec - 1)
        sends = []
        for k, peer in enumerate(everyone):
            copy = pltpu.make_async_remote_copy(
                src_ref=stats.at[c, mine],
                dst_ref=stats.at[c, mine],
                send_sem=sum_send.at[c, k],
                recv_sem=sum_recv.at[c, k],
                device_id=peer,
                device_id_type=MESH,
            )
            copy.start()
            sends.append(copy)
        for copy in sends:
            copy.wait()
        summed = stats[c, 0]
        for k in range(1, n_sec * n_gx):
            summed = summed + stats[c, k]
        parts = [
            jnp.sum(jnp.where(group[0:1] == k, summed, 0.0), axis=1, keepdims=True)
            for k in range(2 * ITERS)
        ]
        x = coefficients(parts[:ITERS], parts[ITERS:])
        x = [jnp.broadcast_to(v, (rows, cols)) for v in x]

        def update(l, carry):
            v = head[l, 0:rows, 0:cols]
            for k in range(ITERS):
                v = v + x[k] * basis[k][l, 0:rows, 0:cols]
            head[l, 0:rows, 0:cols] = v
            return carry

        if c + 1 == steps:
            for i in range(1, n_sec):
                peer = sec_peers[i - 1]
                lax.fori_loop(1 + peer * layers, 1 + (peer + 1) * layers, update, 0)
                back_copy(i - 1, peer).start()
                outgoing.append(back_copy(i - 1, peer))
            lax.fori_loop(1 + sec * layers, 1 + (sec + 1) * layers, update, 0)
        else:
            lax.fori_loop(1, total + 1, update, 0)
        if c + 1 < steps:
            for d in (0, 1):
                @pl.when(gx > 0 if d == 0 else gx < n_gx - 1)
                def _(d=d):
                    for k in range(ITERS):
                        land_copy(k, d).wait_send()

                @pl.when(gx < n_gx - 1 if d == 0 else gx > 0)
                def _(d=d):
                    for k in range(ITERS):
                        land_copy(k, d).wait_recv()

            def update_rim(l, carry):
                for d in (0, 1):
                    at_rows = slice(rows + d * RIM, rows + d * RIM + RIM)
                    v = head[l, at_rows, 0:cols]
                    for k in range(ITERS):
                        v = v + x[k][0:RIM] * landed[c, k, d, l - 1]
                    head[l, at_rows, 0:cols] = v
                return carry

            lax.fori_loop(1, total + 1, update_rim, 0)

    copy = pltpu.make_async_copy(head.at[layers_of(sec), 0:rows, 0:cols], out_ref.at[:, :, at(here)], own_sem.at[2])
    copy.start()
    outgoing.append(copy)
    for copy in outgoing:
        copy.wait()


def body(n_sec, n_gx, start, soil, conductivity, storage, rain):
    layers, rows, wide = start.shape
    steps = rain.shape[0]
    cols = wide // n_sec
    total = layers * n_sec
    assert total * RIM <= LANES and cols % LANES == 0 and rows % RIM == 0 and n_sec == 4
    ext = (rows + 2 * RIM, cols + LANES)
    f32 = jnp.float32
    field = pltpu.VMEM((total + 2,) + ext, f32)
    per_sec = pltpu.VMEM((n_sec,) + ext, f32)
    dma = pltpu.SemaphoreType.DMA
    vmem = pl.BlockSpec(memory_space=pltpu.VMEM)
    hbm = pl.BlockSpec(memory_space=pl.ANY)
    smem = pl.BlockSpec(memory_space=pltpu.SMEM)
    return tuple(pl.pallas_call(
        functools.partial(kernel, n_sec, n_gx, steps, conductivity.shape[0]),
        out_shape=(
            jax.ShapeDtypeStruct(start.shape, f32),
            jax.ShapeDtypeStruct((1, steps, rows, wide), f32),
        ),
        in_specs=[hbm, hbm, smem, smem, vmem],
        out_specs=(hbm, hbm),
        scratch_shapes=[field, pltpu.VMEM((total + 2,) + ext, jnp.int32)]
        + [field] * 13
        + [per_sec] * 3
        + [
            pltpu.VMEM((steps,) + ext, f32),
            pltpu.VMEM((n_sec, steps, rows, cols), f32),
            pltpu.VMEM((steps, 2, ext[0], LANES), f32),
            pltpu.VMEM((steps, 2, ext[0], LANES), f32),
            pltpu.VMEM((2, ext[0], LANES), jnp.int32),
            pltpu.VMEM((2, ext[0], LANES), jnp.int32),
            pltpu.VMEM((steps, ITERS, 2, total, RIM, cols), f32),
            pltpu.VMEM((steps, n_sec * n_gx, 1, LANES), f32),
            pltpu.SemaphoreType.REGULAR,
            dma((3 + steps,)),
            dma((2, n_sec - 1)),
            dma((2, n_sec - 1)),
            dma((steps + 1, 2)),
            dma((steps + 1, 2)),
            dma((3, 2)),
            dma((3, 2)),
            dma((steps, ITERS, 2)),
            dma((steps, ITERS, 2)),
            dma((steps, n_sec * n_gx)),
            dma((steps, n_sec * n_gx)),
            dma((steps, n_sec - 1)),
            dma((steps, n_sec - 1)),
            dma((n_sec - 1,)),
            dma((n_sec - 1,)),
        ],
        compiler_params=pltpu.CompilerParams(collective_id=0, has_side_effects=True),
    )(start, soil, conductivity, storage, rain))


def solution(mesh):
    placed = (P("sec", "gx", None), P("sec", "gx", None), P(), P(), P(None, "gx", None))
    return jax.shard_map(
        functools.partial(body, mesh.shape["sec"], mesh.shape["gx"]),
        mesh=mesh,
        in_specs=placed,
        out_specs=(P("sec", "gx", None), P("sec", None, "gx", None)),
        check_vma=False,
    )
```

profile of v0, /device:TPU:0, one launch (start us, length us, event | category | flops | bytes accessed | tf_op | source)
XLA Modules:
  0.0 81.3 jit_solution(3537371878336261757)
XLA Ops:
  0.6 78.3 %shard_map.68 = (f32[4,16,1024]{2,1,0:T(8,128)}, f32[1,3,16,1024]{3,2,1,0:T(8,128)}) custom-call(f32[4,16,1024]{2,1,0:T(8,128)} %start_ref.1, s32[4,16,1024]{2,1,0:T(8,128)} %soil_ref.1, f32[12]{0:T(128)} %cond_ref.1, f32[12]{0:T(128)} %store_ref.1, f32[3,16,1024]{2,1,0:T(8,128)} %rain_ref.1), custom_call_target="tpu_custom_call" | custom-call | tf_op jit(solution)/shard_map/pallas_call | solution.py:552
  78.9 0.0 copy-start
  78.9 1.7 %copy.9 = f32[4,16,1024]{2,1,0:T(8,128)} copy(f32[4,16,1024]{2,1,0:T(8,128)} %get-tuple-element.4) | data formatting | bytes 524288
  80.6 0.0 copy-done
  80.6 0.7 copy.10
Async XLA Ops:
  78.9 1.7 %copy-start = (f32[1,3,16,1024]{3,2,1,0:T(8,128)S(1)}, f32[1,3,16,1024]{3,2,1,0:T(8,128)}, u32[]{:S(2)}) copy-start(f32[1,3,16,1024]{3,2,1,0:T(8,128)} %get-tuple-element.5) | copy-start | bytes 589828
where the time goes:
time: 81.5 us; the launch traced here: 81.3 us
  Pallas kernels  78.3 us (96%)
  local copies, waits for them, and re-layouts  2.39 us (3%)
    pallas_call x1, Pallas kernels, body(): pl.pallas_call(functools.partial(kernel, n_sec, n_gx, steps, conductivity...  78.3 us
    unnamed x4, local copies, waits for them, and re-layouts  2.39 us

commit v1 on v0

--- a/solution.py
+++ b/solution.py
@@ -12,6 +12,15 @@
 RIM = 8
 LANES = 128
 ITERS = 4
+
+
+def by_group(low, high, each, body, carry):
+    def trip(i, carry):
+        for j in range(each):
+            carry = body(low + i * each + j, carry)
+        return carry
+
+    return lax.fori_loop(0, (high - low) // each, trip, carry)
 
 
 def place_of(s):
@@ -357,10 +366,10 @@
 
         def prepare(lanes):
             if c == 0:
-                lax.fori_loop(1, total + 1, functools.partial(look, lanes), 0)
+                by_group(1, total + 1, layers, functools.partial(look, lanes), 0)
             lax.fori_loop(0, n_sec, functools.partial(soil, lanes), 0)
             couple(lanes)
-            lax.fori_loop(1, total + 1, functools.partial(faces, lanes), 0)
+            by_group(1, total + 1, layers, functools.partial(faces, lanes), 0)
 
         prepare(slice(0, cols))
         own_flow = pltpu.make_async_copy(flows.at[sec, c], flow_ref.at[0, c, :, at(here)], own_sem.at[3 + c])
@@ -383,7 +392,7 @@
             take_cols(steps, soils)
         take_cols(c, head)
         prepare(slice(cols, ext_c))
-        lax.fori_loop(1, total + 1, faces_across, 0)
+        by_group(1, total + 1, layers, faces_across, 0)
 
         def first(s, acc):
             for j in range(layers):
@@ -447,7 +456,7 @@
                     ag = ag + folded(diag[l] * new * new)
                 return (ah, ag)
 
-            ah, ag = lax.fori_loop(1, total + 1, apply, (none, none))
+            ah, ag = by_group(1, total + 1, layers, apply, (none, none))
             h.append(ah)
             if k + 1 < ITERS:
                 g.append(ag)
@@ -504,7 +513,7 @@
                 outgoing.append(back_copy(i - 1, peer))
             lax.fori_loop(1 + sec * layers, 1 + (sec + 1) * layers, update, 0)
         else:
-            lax.fori_loop(1, total + 1, update, 0)
+            by_group(1, total + 1, layers, update, 0)
         if c + 1 < steps:
             for d in (0, 1):
                 @pl.when(gx > 0 if d == 0 else gx < n_gx - 1)
@@ -526,7 +535,7 @@
                     head[l, at_rows, 0:cols] = v
                 return carry
 
-            lax.fori_loop(1, total + 1, update_rim, 0)
+            by_group(1, total + 1, layers, update_rim, 0)
 
     copy = pltpu.make_async_copy(head.at[layers_of(sec), 0:rows, 0:cols], out_ref.at[:, :, at(here)], own_sem.at[2])
     copy.start()

time: 81.5 us -> 71.3 us (0.87)
  Pallas kernels: 78.3 us -> 68.1 us
    pallas_call x1, Pallas kernels: 78.3 us -> 68.1 us  [body(): pl.pallas_call(functools.partial(kernel, n_sec, n_gx, steps, conductivity...]
where the time goes in v1:
time: 71.3 us; the launch traced here: 71.1 us
  Pallas kernels  68.1 us (96%)
  local copies, waits for them, and re-layouts  2.39 us (3%)
    pallas_call x1, Pallas kernels, body(): pl.pallas_call(functools.partial(kernel, n_sec, n_gx, steps, conductivity...  68.1 us
    unnamed x4, local copies, waits for them, and re-layouts  2.39 us

profile of v1, /device:TPU:0, one launch (start us, length us, event | category | flops | bytes accessed | tf_op | source)
XLA Modules:
  0.0 71.1 jit_solution(10803132592824417258)
XLA Ops:
  0.6 68.1 %shard_map.68 = (f32[4,16,1024]{2,1,0:T(8,128)}, f32[1,3,16,1024]{3,2,1,0:T(8,128)}) custom-call(f32[4,16,1024]{2,1,0:T(8,128)} %start_ref.1, s32[4,16,1024]{2,1,0:T(8,128)} %soil_ref.1, f32[12]{0:T(128)} %cond_ref.1, f32[12]{0:T(128)} %store_ref.1, f32[3,16,1024]{2,1,0:T(8,128)} %rain_ref.1), custom_call_target="tpu_custom_call" | custom-call | tf_op jit(solution)/shard_map/pallas_call | solution.py:561
  68.7 0.0 copy-start
  68.7 1.7 %copy.9 = f32[4,16,1024]{2,1,0:T(8,128)} copy(f32[4,16,1024]{2,1,0:T(8,128)} %get-tuple-element.4) | data formatting | bytes 524288
  70.4 0.0 copy-done
  70.4 0.7 copy.10
Async XLA Ops:
  68.7 1.7 %copy-start = (f32[1,3,16,1024]{3,2,1,0:T(8,128)S(1)}, f32[1,3,16,1024]{3,2,1,0:T(8,128)}, u32[]{:S(2)}) copy-start(f32[1,3,16,1024]{3,2,1,0:T(8,128)} %get-tuple-element.5) | copy-start | bytes 589828

commit v2 on v1

v2 whole, which is shorter than its diff:
```python
import functools

import jax
import jax.numpy as jnp
from jax import lax
from jax.experimental import pallas as pl
from jax.experimental.pallas import tpu as pltpu
from jax.sharding import PartitionSpec as P


MESH = pl.DeviceIdType.MESH
RIM = 8
LANES = 128
ITERS = 4
LOW = RIM // 2


def by_group(low, high, each, body, carry):
    def trip(i, carry):
        for j in range(each):
            carry = body(low + i * each + j, carry)
        return carry

    return lax.fori_loop(0, (high - low) // each, trip, carry)


def place_of(s):
    return s + s // 2 - 2 * (s // 3)


def mirrored(a, mask, count):
    out, bit = 0, 1
    while bit < count:
        out = out + lax.rem(a // bit + (mask // bit) % 2, 2) * bit
        bit *= 2
    return out


def coefficients(g, h):
    nu = [g[0], h[0]]
    for k in range(1, ITERS):
        nu.append(2.0 * g[k] - nu[0])
        nu.append(4.0 * h[k] - 2.0 * nu[1] - nu[2 * k - 1])

    def gram(i, j):
        return 0.5 * (nu[i + j] + nu[abs(i - j)])

    def gram_a(i, j):
        shifted = gram(i, 1) if j == 0 else 0.5 * (gram(i, j + 1) + gram(i, j - 1))
        return gram(i, j) - shifted

    G = [[gram(i, j) for j in range(ITERS)] for i in range(ITERS)]
    H = [[gram_a(max(i, j), min(i, j)) for j in range(ITERS)] for i in range(ITERS)]
    zero = jnp.zeros_like(g[0])

    def form(matrix, v, top):
        total = zero
        for i in range(top + 1):
            row = matrix[i][i] * v[i]
            for j in range(i):
                row = row + 2.0 * matrix[i][j] * v[j]
            total = total + row * v[i]
        return total

    z = [zero + 1.0] + [zero] * (ITERS - 1)
    p = list(z)
    x = [zero] * ITERS
    rz = nu[0]
    for k in range(ITERS):
        curve = form(H, p, k)
        alpha = jnp.where(curve > 0.0, rz / jnp.where(curve > 0.0, curve, 1.0), 0.0)
        x = [a + alpha * b for a, b in zip(x, p)]
        if k + 1 < ITERS:
            image = list(p)
            for i in range(k + 1):
                if i == 0:
                    image[1] = image[1] - p[0]
                else:
                    image[i + 1] = image[i + 1] - 0.5 * p[i]
                    image[i - 1] = image[i - 1] - 0.5 * p[i]
            z = [a - alpha * b for a, b in zip(z, image)]
            new = jnp.maximum(form(G, z, k + 1), 0.0)
            beta = jnp.where(rz > 0.0, new / jnp.where(rz > 0.0, rz, 1.0), 0.0)
            p = [a + beta * b for a, b in zip(z, p)]
            rz = new
    return x


def kernel(
    n_sec, n_gx, steps, kinds,
    start_ref, soil_ref, cond_ref, store_ref, rain_ref,
    out_ref, flow_ref,
    head, soils, kind, store, cond, cap, face_l, face_r, face_c, diag, dinv, t0, t1, t2, t3,
    water, enter, leave, rainx, flows, pack_out, pack_in, edge_f, edge_i, edges_f, edges_i,
    stage_f, stage_i, stage_r, rows_out, landed, stats,
    met_sem, own_sem, load_sem, swap_send, swap_recv, row_send, row_recv, rain_send, rain_recv,
    col_send, col_recv, land_send, land_recv, sum_send, sum_recv, flow_send, flow_recv, back_send, back_recv,
):
    f32 = jnp.float32
    layers, rows, wide = start_ref.shape
    cols = wide // n_sec
    tiles = cols // LANES
    total = layers * n_sec
    ext = rows + 2 * RIM
    sec, gx = lax.axis_index("sec"), lax.axis_index("gx")
    here = place_of(sec)
    own = slice(RIM, RIM + rows)
    work = slice(LOW, ext - LOW)
    above = slice(LOW - 1, ext - LOW - 1)
    under = slice(LOW + 1, ext - LOW + 1)
    everywhere = list(range(tiles + 1))
    inner = list(range(tiles))

    def lanes_at(place, tile):
        return pl.ds(pl.multiple_of(place * cols + tile * LANES, LANES), LANES)

    def layers_of(s):
        return pl.ds(1 + s * layers, layers)

    sec_peers = [lax.rem(sec + k, n_sec) for k in range(1, n_sec)]
    sec_froms = [lax.rem(sec + n_sec - k, n_sec) for k in range(n_sec)]
    gx_peers = [lax.rem(gx + k, n_gx) for k in range(1, n_gx)]
    everyone = [
        {"sec": mirrored(sec, i, n_sec), "gx": mirrored(gx, j, n_gx)}
        for j in reversed(range(n_gx)) for i in reversed(range(n_sec)) if i + j
    ]

    loads = [
        pltpu.make_async_copy(src, dst, load_sem.at[f])
        for f, (src, dst) in enumerate(((start_ref, stage_f), (soil_ref, stage_i), (rain_ref, stage_r)))
    ]
    for copy in loads:
        copy.start()
    barrier = pltpu.get_barrier_semaphore()
    for peer in sec_peers:
        pl.semaphore_signal(barrier, inc=1, device_id={"sec": peer}, device_id_type=MESH)
    for peer in gx_peers:
        pl.semaphore_signal(barrier, inc=1, device_id={"gx": peer}, device_id_type=MESH)

    def nil(*shape, dtype=f32):
        return jnp.zeros(shape, dtype)

    for ref in (head, cond, t0, t1, t2, t3, face_l):
        ref[0] = nil(tiles + 1, ext, LANES)
        ref[total + 1] = nil(tiles + 1, ext, LANES)

    def hem(l, carry):
        for ref in (t0, t1, t2, t3, face_r):
            ref[l, :, 0:RIM] = nil(tiles + 1, RIM, LANES)
            ref[l, :, ext - RIM:ext] = nil(tiles + 1, RIM, LANES)
        return carry

    lax.fori_loop(1, total + 1, hem, 0)
    for d in (0, 1):
        rim = slice(ext - RIM, ext) if d == 0 else slice(0, RIM)

        @pl.when(gx == n_gx - 1 if d == 0 else gx == 0)
        def _(d=d, rim=rim):
            def wipe(l, carry):
                head[l + 1, :, rim] = nil(tiles + 1, RIM, LANES)
                soils[l + 1, :, rim] = nil(tiles + 1, RIM, LANES, dtype=jnp.int32)
                return carry

            lax.fori_loop(0, total, wipe, 0)
            for c in range(steps):
                rainx[c, :, rim] = nil(tiles + 1, RIM, LANES)
            edge_f[:, rim] = nil(n_sec, RIM, LANES)
            edge_i[:, rim] = nil(n_sec, RIM, LANES, dtype=jnp.int32)
            for c in range(steps - 1):
                for k in range(ITERS):
                    landed[c, k, d] = nil(total // 2, tiles, RIM, LANES)

        @pl.when(here == n_sec - 1 if d == 0 else here == 0)
        def _(d=d):
            for c in range(steps - 1):
                pack_in[c, d] = nil(ext, LANES)

    lane = lax.broadcasted_iota(jnp.int32, (ext, LANES), 1)
    lane_w = lax.broadcasted_iota(jnp.int32, (rows + RIM, LANES), 1)
    lane_o = lax.broadcasted_iota(jnp.int32, (rows, LANES), 1)
    at_row = lax.broadcasted_iota(jnp.int32, (ext, LANES), 0)
    beyond = ((at_row >= rows + RIM) & (gx == n_gx - 1)) | ((at_row < RIM) & (gx == 0))
    beside = (lane >= RIM) & (lane < LANES - RIM)
    beside = beside | ((lane < RIM) & (here == n_sec - 1)) | ((lane >= LANES - RIM) & (here == 0))
    outside = [beyond] * tiles + [beyond | beside]

    for copy in loads:
        copy.wait()

    after = lanes_at(lax.rem(here + 1, n_sec), 0)
    before = lanes_at(lax.rem(here + n_sec - 1, n_sec), tiles - 1)
    for c in range(steps):
        for ct in inner:
            rainx[c, ct, own] = stage_r[c, :, lanes_at(here, ct)]
        rainx[c, tiles, own] = jnp.where(lane_o < LANES // 2, stage_r[c, :, after], stage_r[c, :, before])
    for stage, edges in ((stage_f, edges_f), (stage_i, edges_i)):
        for place in range(n_sec):
            out = nil(rows, LANES, dtype=stage.dtype)
            for j in range(layers):
                right = nil(rows, LANES, dtype=stage.dtype)
                left = right
                if place + 1 < n_sec:
                    right = stage[j, :, (place + 1) * cols:(place + 1) * cols + LANES]
                if place > 0:
                    left = stage[j, :, place * cols - LANES:place * cols]
                both = jnp.where(lane_o < RIM, right, left)
                moved = pltpu.roll(both, (2 * RIM * j + RIM) % LANES, 1)
                out = jnp.where(lane_o // (2 * RIM) == j, moved, out)
            edges[place] = out

    pl.semaphore_wait(barrier, n_sec + n_gx - 2)
    for peer in sec_peers:
        pl.semaphore_signal(met_sem, inc=1, device_id={"sec": peer}, device_id_type=MESH)

    parcels = ((stage_i, soils, edges_i, edge_i), (stage_f, head, edges_f, edge_f))
    swaps = [[] for _ in range(n_sec)]
    for f, (stage, field, edges, edge) in enumerate(parcels):
        for ct in inner:
            swaps[0].append(pltpu.make_async_copy(
                stage.at[:, :, lanes_at(here, ct)], field.at[layers_of(sec), ct, own], own_sem.at[f, ct]
            ))
        swaps[0].append(pltpu.make_async_copy(edges.at[here], edge.at[sec, own], own_sem.at[f, tiles]))
    for k, peer in enumerate(sec_peers):
        for f, (stage, field, edges, edge) in enumerate(parcels):
            moves = [
                (stage.at[:, :, lanes_at(place_of(peer), ct)], field.at[layers_of(sec), ct, own]) for ct in inner
            ]
            moves.append((edges.at[place_of(peer)], edge.at[sec, own]))
            for m, (src, dst) in enumerate(moves):
                swaps[k + 1].append(pltpu.make_async_remote_copy(
                    src_ref=src,
                    dst_ref=dst,
                    send_sem=swap_send.at[k, f, m],
                    recv_sem=swap_recv.at[k, f, m],
                    device_id={"sec": peer},
                    device_id_type=MESH,
                ))
    for moves in swaps:
        for copy in moves:
            copy.start()

    def toward(d):
        return lax.rem(gx + n_gx - 1, n_gx) if d == 0 else lax.rem(gx + 1, n_gx)

    def ends(d):
        return (slice(RIM, 2 * RIM), slice(ext - RIM, ext)) if d == 0 else (slice(rows, rows + RIM), slice(0, RIM))

    def sends_to(d):
        return gx > 0 if d == 0 else gx < n_gx - 1

    def rain_copy(d):
        src, dst = ends(d)
        return pltpu.make_async_remote_copy(
            src_ref=rainx.at[:, :, src],
            dst_ref=rainx.at[:, :, dst],
            send_sem=rain_send.at[d],
            recv_sem=rain_recv.at[d],
            device_id={"gx": toward(d)},
            device_id_type=MESH,
        )

    def row_copies(k, d):
        src, dst = ends(d)
        s = sec_froms[k]
        copies = []
        for f, (_, field, _, edge) in enumerate(parcels):
            pairs = ((field.at[layers_of(s), 0:tiles, src], field.at[layers_of(s), 0:tiles, dst]),
                     (edge.at[s, src], edge.at[s, dst]))
            for m, (a, b) in enumerate(pairs):
                copies.append(pltpu.make_async_remote_copy(
                    src_ref=a,
                    dst_ref=b,
                    send_sem=row_send.at[k, f, d, m],
                    recv_sem=row_recv.at[k, f, d, m],
                    device_id={"gx": toward(d)},
                    device_id_type=MESH,
                ))
        return copies

    for d in (0, 1):
        @pl.when(sends_to(d))
        def _(d=d):
            rain_copy(d).start()

    for k in range(n_sec):
        for copy in swaps[k]:
            copy.wait()
        for d in (0, 1):
            @pl.when(sends_to(d))
            def _(d=d, k=k):
                for copy in row_copies(k, d):
                    copy.start()

    def take_rows(k):
        for d in (0, 1):
            @pl.when(sends_to(d))
            def _(d=d):
                for copy in row_copies(k, d):
                    copy.wait_send()
                for copy in row_copies(k, 1 - d):
                    copy.wait_recv()

    def packed(tile, low):
        outs = nil(ext, LANES)
        for l in range(total):
            shift = (RIM * l if low else RIM * l + RIM) % LANES
            piece = head[1 + l, tile]
            moved = pltpu.roll(piece, shift, 1) if shift else piece
            outs = jnp.where(lane // RIM == l, moved, outs)
        return outs

    def col_copy(c, d):
        return pltpu.make_async_remote_copy(
            src_ref=pack_out.at[c, d],
            dst_ref=pack_in.at[c, d],
            send_sem=col_send.at[c, d],
            recv_sem=col_recv.at[c, d],
            device_id={"sec": place_of(lax.rem(here + n_sec - 1, n_sec) if d == 0 else lax.rem(here + 1, n_sec))},
            device_id_type=MESH,
        )

    def send_cols(c):
        for d in (0, 1):
            @pl.when(here > 0 if d == 0 else here < n_sec - 1)
            def _(d=d):
                pack_out[c, d] = packed(0 if d == 0 else tiles - 1, d == 0)
                col_copy(c, d).start()

    def take_cols(c):
        @pl.when(here > 0)
        def _():
            col_copy(c, 0).wait_send()
            col_copy(c, 1).wait_recv()

        @pl.when(here < n_sec - 1)
        def _():
            col_copy(c, 1).wait_send()
            col_copy(c, 0).wait_recv()

        right, left = pack_in[c, 0], pack_in[c, 1]
        for l in range(total):
            a, b = (-RIM * l) % LANES, (LANES - RIM - RIM * l) % LANES
            ra = pltpu.roll(right, a, 1) if a else right
            rb = pltpu.roll(left, b, 1) if b else left
            head[1 + l, tiles] = jnp.where(lane < RIM, ra, jnp.where(lane >= LANES - RIM, rb, 0.0))

    def right_of(v, at):
        moved = [pltpu.roll(a, LANES - 1, 1) for a in v]
        return [jnp.where(at == LANES - 1, moved[(i + 1) % len(v)], moved[i]) for i in range(len(v))]

    def left_of(v, at):
        moved = [pltpu.roll(a, 1, 1) for a in v]
        return [jnp.where(at == 0, moved[i - 1], moved[i]) for i in range(len(v))]

    def harmonic(a, b):
        return 2.0 * a * b / jnp.maximum(a + b, 1e-30)

    half = lax.broadcasted_iota(jnp.int32, (RIM, LANES), 0) >= LOW

    def own_of(v):
        out = jnp.where(half, v[0:RIM], v[rows:rows + RIM])
        for i in range(RIM, rows, RIM):
            out = out + v[i:i + RIM]
        return out

    none = nil(RIM, LANES)
    basis = (t0, t1, t2, t3)

    def back_copies(k, peer):
        return [
            pltpu.make_async_remote_copy(
                src_ref=head.at[layers_of(peer), ct, own],
                dst_ref=out_ref.at[:, :, lanes_at(here, ct)],
                send_sem=back_send.at[k, ct],
                recv_sem=back_recv.at[k, ct],
                device_id={"sec": peer},
                device_id_type=MESH,
            )
            for ct in inner
        ]

    def soil(which, s):
        for ct in which:
            amount = nil(ext, LANES)
            for j in range(layers):
                l = 1 + s * layers + j
                sat = jax.nn.sigmoid(head[l, ct])
                cond[l, ct] = kind[l, ct] * (0.05 + sat * sat)
                cap[l, ct] = store[l, ct] * (0.1 + sat * (1.0 - sat))
                amount = amount + sat
            water[s, ct] = amount

    spot = lax.broadcasted_iota(jnp.int32, (ext, LANES), 1)
    of_cond = nil(ext, LANES)
    of_store = nil(ext, LANES)
    for k in range(kinds):
        of_cond = jnp.where(spot == k, cond_ref[k], of_cond)
        of_store = jnp.where(spot == k, store_ref[k], of_store)

    def open_edges(s):
        for edge, field in ((edge_f, head), (edge_i, soils)):
            taken = edge[s]
            for j in range(layers):
                moved = pltpu.roll(taken, LANES - RIM - 2 * RIM * j, 1)
                field[1 + s * layers + j, tiles] = jnp.where(
                    (lane < RIM) | (lane >= LANES - RIM), moved, nil(ext, LANES, dtype=field.dtype)
                )

    def look(s):
        for j in range(layers):
            l = 1 + s * layers + j
            for ct in everywhere:
                which = soils[l, ct]
                a = jnp.take_along_axis(of_cond, which, axis=1, mode="promise_in_bounds")
                b = jnp.take_along_axis(of_store, which, axis=1, mode="promise_in_bounds")
                kind[l, ct] = jnp.where(outside[ct], 0.0, a)
                store[l, ct] = jnp.where(outside[ct], 0.0, b)

    outgoing = []
    for c in range(steps):
        def couple(which, c=c):
            depth = jnp.float32(layers)
            for ct in which:
                below = nil(ext, LANES)
                slopes = [None] * n_sec
                for s in reversed(range(n_sec)):
                    amount = water[s, ct]
                    slopes[s] = amount / depth * (0.5 + 0.5 * below / (below + depth))
                    below = below + amount
                entering = rainx[c, ct]
                for s in range(n_sec):
                    enter[s, ct] = entering
                    if ct < tiles:
                        flows[s, c, :, ct * LANES:(ct + 1) * LANES] = entering[own]
                    entering = slopes[s] * entering + 0.5 * cond[(s + 1) * layers, ct]
                    leave[s, ct] = entering

        def faces(which, l, carry):
            for ct in which:
                k = cond[l, ct, work]
                face_l[l, ct, work] = harmonic(k, cond[l + 1, ct, work])
                face_r[l, ct, work] = harmonic(k, cond[l, ct, under])
            return carry

        def faces_across(l, carry):
            k = [cond[l, ct, work] for ct in everywhere]
            for ct, other in zip(everywhere, right_of(k, lane_w)):
                face_c[l, ct, work] = harmonic(k[ct], other)
            return carry

        def prepare(which, c=c):
            if c > 0:
                def each(s, carry):
                    soil(which, s)
                    return carry

                lax.fori_loop(0, n_sec, each, 0)
            couple(which)
            by_group(1, total + 1, layers, functools.partial(faces, which), 0)

        if c == 0:
            for k in range(n_sec):
                s = sec_froms[k]
                take_rows(k)
                open_edges(s)
                look(s)
                soil(everywhere, s)
            for d in (0, 1):
                @pl.when(sends_to(d))
                def _(d=d):
                    rain_copy(d).wait_send()
                    rain_copy(1 - d).wait_recv()
        else:
            send_cols(c - 1)

        prepare(inner)
        own_flow = pltpu.make_async_copy(
            flows.at[sec, c], flow_ref.at[0, c, :, pl.ds(pl.multiple_of(here * cols, LANES), cols)], flow_send.at[c, n_sec - 1]
        )
        own_flow.start()
        late = [own_flow]
        for k, peer in enumerate(sec_peers):
            copy = pltpu.make_async_remote_copy(
                src_ref=flows.at[peer, c],
                dst_ref=flow_ref.at[0, c, :, pl.ds(pl.multiple_of(here * cols, LANES), cols)],
                send_sem=flow_send.at[c, k],
                recv_sem=flow_recv.at[c, k],
                device_id={"sec": peer},
                device_id_type=MESH,
            )
            copy.start()
            late.append(copy)
        outgoing += late

        if c > 0:
            take_cols(c - 1)
        prepare([tiles])
        by_group(1, total + 1, layers, faces_across, 0)

        def rows_of(k, l, m):
            if c + 1 < steps:
                i = (l - 1) // 2
                for ct in inner:
                    for j in (0, 1):
                        put = slice(j * LOW, j * LOW + LOW)
                        rows_out[k, 0, i, ct, put] = basis[k][l + j, ct, RIM + 1:RIM + 1 + LOW]
                        rows_out[k, 1, i, ct, put] = basis[k][l + j, ct, RIM + rows - LOW:RIM + rows]

        def first(s, acc):
            for j in range(layers):
                l = 1 + s * layers + j
                fc = [face_c[l, ct, work] for ct in everywhere]
                v = [head[l, ct, work] for ct in everywhere]
                flux = [a * (b - d) for a, b, d in zip(fc, right_of(v, lane_w), v)]
                fb, back = left_of(fc, lane_w), left_of(flux, lane_w)
                for ct in everywhere:
                    up, down = face_l[l - 1, ct, work], face_l[l, ct, work]
                    fr, fa = face_r[l, ct, work], face_r[l, ct, above]
                    whole = cap[l, ct, work] + up + down + fr + fa + fc[ct] + fb[ct]
                    res = up - down + up * (head[l - 1, ct, work] - v[ct]) + down * (head[l + 1, ct, work] - v[ct])
                    res = res + fr * (head[l, ct, under] - v[ct]) + fa * (head[l, ct, above] - v[ct])
                    res = res + flux[ct] - back[ct]
                    if j == 0:
                        res = res + enter[s, ct, work]
                    if j == layers - 1:
                        res = res - leave[s, ct, work]
                    inverse = jnp.where(whole > 0.0, 1.0 / jnp.maximum(whole, 1e-30), 0.0)
                    z = res * inverse
                    diag[l, ct, work] = whole
                    dinv[l, ct, work] = 2.0 * inverse
                    t0[l, ct, work] = z
                    if ct < tiles:
                        acc = acc + own_of(res * z)
            for j in range(0, layers, 2):
                rows_of(0, 1 + s * layers + j, s)
            return acc

        def land_copy(k, d, c=c):
            return pltpu.make_async_remote_copy(
                src_ref=rows_out.at[k, d],
                dst_ref=landed.at[c, k, d],
                send_sem=land_send.at[c, k, d],
                recv_sem=land_recv.at[c, k, d],
                device_id={"gx": toward(d)},
                device_id_type=MESH,
            )

        def send_land(k):
            if c + 1 < steps:
                for d in (0, 1):
                    @pl.when(sends_to(d))
                    def _(d=d):
                        land_copy(k, d).start()

        g = [lax.fori_loop(0, n_sec, first, none)]
        send_land(0)
        h = []
        for k in range(ITERS - 1):
            def apply(i, acc, k=k):
                t = basis[k]
                for j in range(layers):
                    l = 1 + i * layers + j
                    v = [t[l, ct, work] for ct in everywhere]
                    fc = [face_c[l, ct, work] for ct in everywhere]
                    aside = right_of(v, lane_w)
                    back = left_of([a * b for a, b in zip(fc, v)], lane_w)
                    for ct in everywhere:
                        near = face_l[l - 1, ct, work] * t[l - 1, ct, work] + face_l[l, ct, work] * t[l + 1, ct, work]
                        near = near + face_r[l, ct, work] * t[l, ct, under] + face_r[l, ct, above] * t[l, ct, above]
                        near = near + (fc[ct] * aside[ct] + back[ct])
                        new = dinv[l, ct, work] * near
                        new = 0.5 * new if k == 0 else new - basis[k - 1][l, ct, work]
                        basis[k + 1][l, ct, work] = new
                        if ct < tiles:
                            acc = (acc[0] + own_of(v[ct] * near), acc[1] + own_of(diag[l, ct, work] * new * new))
                for j in range(0, layers, 2):
                    rows_of(k + 1, 1 + i * layers + j, i)
                return acc

            ah, ag = lax.fori_loop(0, n_sec, apply, (none, none))
            h.append(ah)
            g.append(ag)
            send_land(k + 1)

        def last(l, acc):
            t = basis[ITERS - 1]
            v = [t[l, ct, own] for ct in everywhere]
            aside = right_of(v, lane_o)
            for ct in inner:
                near = face_l[l, ct, own] * t[l + 1, ct, own] + face_c[l, ct, own] * aside[ct]
                near = v[ct] * (near + face_r[l, ct, own] * t[l, ct, RIM + 1:RIM + rows + 1])
                for i in range(0, rows, RIM):
                    acc = acc + near[i:i + RIM]
            return acc

        h.append(2.0 * by_group(1, total + 1, layers, last, none))

        flat = jnp.concatenate([jnp.sum(v, axis=0, keepdims=True) for v in g + h], axis=0)
        part = LANES // (2 * ITERS)
        by = LANES // 2
        while by >= part:
            flat = flat + pltpu.roll(flat, by, 1)
            by //= 2
        which = lax.broadcasted_iota(jnp.int32, flat.shape, 0)
        group = lax.broadcasted_iota(jnp.int32, flat.shape, 1) // part
        mine = sec * n_gx + gx
        stats[c, mine] = jnp.sum(jnp.where(which == group, flat, 0.0), axis=0, keepdims=True)
        if c == 0:
            pl.semaphore_wait(met_sem, n_sec - 1)
        sends = []
        for k, peer in enumerate(everyone):
            copy = pltpu.make_async_remote_copy(
                src_ref=stats.at[c, mine],
                dst_ref=stats.at[c, mine],
                send_sem=sum_send.at[c, k],
                recv_sem=sum_recv.at[c, k],
                device_id=peer,
                device_id_type=MESH,
            )
            copy.start()
            sends.append(copy)
        for copy in sends:
            copy.wait()
        summed = stats[c, 0]
        for k in range(1, n_sec * n_gx):
            summed = summed + stats[c, k]
        parts = [
            jnp.sum(jnp.where(group[0:1] == k, summed, 0.0), axis=1, keepdims=True)
            for k in range(2 * ITERS)
        ]
        x = coefficients(parts[:ITERS], parts[ITERS:])
        x = [jnp.broadcast_to(v, (rows, LANES)) for v in x]

        def update(l, carry):
            for ct in inner:
                v = head[l, ct, own]
                for k in range(ITERS):
                    v = v + x[k] * basis[k][l, ct, own]
                head[l, ct, own] = v
                if c + 1 < steps:
                    v = head[l, ct, RIM + rows:RIM + rows + 1]
                    for k in range(ITERS):
                        v = v + x[k][0:1] * basis[k][l, ct, RIM + rows:RIM + rows + 1]
                    head[l, ct, RIM + rows:RIM + rows + 1] = v
            return carry

        if c + 1 == steps:
            for i in range(1, n_sec):
                peer = sec_peers[i - 1]
                by_group(1 + peer * layers, 1 + (peer + 1) * layers, layers, update, 0)
                for copy in back_copies(i - 1, peer):
                    copy.start()
                    outgoing.append(copy)
            by_group(1 + sec * layers, 1 + (sec + 1) * layers, layers, update, 0)
        else:
            by_group(1, total + 1, layers, update, 0)
            for d in (0, 1):
                @pl.when(sends_to(d))
                def _(d=d):
                    for k in range(ITERS):
                        land_copy(k, d).wait_send()
                    for k in range(ITERS):
                        land_copy(k, 1 - d).wait_recv()

            def update_rim(i, carry):
                for d in (0, 1):
                    first_row = RIM + rows + 1 if d == 0 else RIM - LOW
                    at_rows = slice(first_row, first_row + LOW)
                    for ct in inner:
                        for j in (0, 1):
                            v = head[1 + 2 * i + j, ct, at_rows]
                            for k in range(ITERS):
                                v = v + x[k][0:LOW] * landed[c, k, d, i, ct, j * LOW:j * LOW + LOW]
                            head[1 + 2 * i + j, ct, at_rows] = v
                return carry

            by_group(0, total // 2, 2, update_rim, 0)

    for ct in inner:
        copy = pltpu.make_async_copy(
            head.at[layers_of(sec), ct, own], out_ref.at[:, :, lanes_at(here, ct)], back_send.at[n_sec - 1, ct]
        )
        copy.start()
        outgoing.append(copy)
    for copy in outgoing:
        copy.wait()


def body(n_sec, n_gx, start, soil, conductivity, storage, rain):
    layers, rows, wide = start.shape
    steps = rain.shape[0]
    cols = wide // n_sec
    tiles = cols // LANES
    total = layers * n_sec
    assert total * RIM <= LANES and cols % LANES == 0 and rows % RIM == 0 and n_sec == 4
    assert layers * 2 * RIM <= LANES and layers % 2 == 0 and n_gx & (n_gx - 1) == 0
    ext = rows + 2 * RIM
    f32, i32 = jnp.float32, jnp.int32
    field = pltpu.VMEM((total + 2, tiles + 1, ext, LANES), f32)
    per_sec = pltpu.VMEM((n_sec, tiles + 1, ext, LANES), f32)
    dma = pltpu.SemaphoreType.DMA
    hbm = pl.BlockSpec(memory_space=pl.ANY)
    smem = pl.BlockSpec(memory_space=pltpu.SMEM)
    return tuple(pl.pallas_call(
        functools.partial(kernel, n_sec, n_gx, steps, conductivity.shape[0]),
        out_shape=(
            jax.ShapeDtypeStruct(start.shape, f32),
            jax.ShapeDtypeStruct((1, steps, rows, wide), f32),
        ),
        in_specs=[hbm, hbm, smem, smem, hbm],
        out_specs=(hbm, hbm),
        scratch_shapes=[field, pltpu.VMEM((total + 2, tiles + 1, ext, LANES), i32)]
        + [field] * 13
        + [per_sec] * 3
        + [
            pltpu.VMEM((steps, tiles + 1, ext, LANES), f32),
            pltpu.VMEM((n_sec, steps, rows, cols), f32),
            pltpu.VMEM((steps - 1, 2, ext, LANES), f32),
            pltpu.VMEM((steps - 1, 2, ext, LANES), f32),
            pltpu.VMEM((n_sec, ext, LANES), f32),
            pltpu.VMEM((n_sec, ext, LANES), i32),
            pltpu.VMEM((n_sec, rows, LANES), f32),
            pltpu.VMEM((n_sec, rows, LANES), i32),
            pltpu.VMEM(start.shape, f32),
            pltpu.VMEM(start.shape, i32),
            pltpu.VMEM(rain.shape, f32),
            pltpu.VMEM((ITERS, 2, total // 2, tiles, RIM, LANES), f32),
            pltpu.VMEM((steps - 1, ITERS, 2, total // 2, tiles, RIM, LANES), f32),
            pltpu.VMEM((steps, n_sec * n_gx, 1, LANES), f32),
            pltpu.SemaphoreType.REGULAR,
            dma((2, tiles + 1)),
            dma((3,)),
            dma((n_sec - 1, 2, tiles + 1)),
            dma((n_sec - 1, 2, tiles + 1)),
            dma((n_sec, 2, 2, 2)),
            dma((n_sec, 2, 2, 2)),
            dma((2,)),
            dma((2,)),
            dma((steps - 1, 2)),
            dma((steps - 1, 2)),
            dma((steps - 1, ITERS, 2)),
            dma((steps - 1, ITERS, 2)),
            dma((steps, n_sec * n_gx)),
            dma((steps, n_sec * n_gx)),
            dma((steps, n_sec)),
            dma((steps, n_sec)),
            dma((n_sec, tiles)),
            dma((n_sec, tiles)),
        ],
        compiler_params=pltpu.CompilerParams(collective_id=0, has_side_effects=True),
    )(start, soil, conductivity, storage, rain))


def solution(mesh):
    placed = (P("sec", "gx", None), P("sec", "gx", None), P(), P(), P(None, "gx", None))
    return jax.shard_map(
        functools.partial(body, mesh.shape["sec"], mesh.shape["gx"]),
        mesh=mesh,
        in_specs=placed,
        out_specs=(P("sec", "gx", None), P("sec", None, "gx", None)),
        check_vma=False,
    )
```

time: 71.3 us -> 62.5 us (0.88)
  Pallas kernels: 68.1 us -> 59.3 us
    pallas_call x1, Pallas kernels: 68.1 us -> 59.3 us  [body(): pl.pallas_call(functools.partial(kernel, n_sec, n_gx, steps, conductivity...]
where the time goes in v2:
time: 62.5 us; the launch traced here: 62.3 us
  Pallas kernels  59.3 us (95%)
  local copies, waits for them, and re-layouts  2.39 us (4%)
  between operations  0.65 us (1%)
    pallas_call x1, Pallas kernels, body(): pl.pallas_call(functools.partial(kernel, n_sec, n_gx, steps, conductivity...  59.3 us
    unnamed x4, local copies, waits for them, and re-layouts  2.39 us

profile of v2, /device:TPU:0, one launch (start us, length us, event | category | flops | bytes accessed | tf_op | source)
XLA Modules:
  0.0 62.3 jit_solution(8224935593369229579)
XLA Ops:
  0.6 59.3 %shard_map.68 = (f32[4,16,1024]{2,1,0:T(8,128)}, f32[1,3,16,1024]{3,2,1,0:T(8,128)}) custom-call(f32[4,16,1024]{2,1,0:T(8,128)} %start_ref.1, s32[4,16,1024]{2,1,0:T(8,128)} %soil_ref.1, f32[12]{0:T(128)} %cond_ref.1, f32[12]{0:T(128)} %store_ref.1, f32[3,16,1024]{2,1,0:T(8,128)} %rain_ref.1), custom_call_target="tpu_custom_call" | custom-call | tf_op jit(solution)/shard_map/pallas_call | solution.py:704
  59.9 0.0 copy-start
  59.9 1.7 %copy.9 = f32[4,16,1024]{2,1,0:T(8,128)} copy(f32[4,16,1024]{2,1,0:T(8,128)} %get-tuple-element.4) | data formatting | bytes 524288
  61.6 0.0 copy-done
  61.6 0.7 %copy.10 = f32[1,3,16,1024]{3,2,1,0:T(8,128)} copy(f32[1,3,16,1024]{3,2,1,0:T(8,128)S(1)} %copy-done) | data formatting | bytes 393216
Async XLA Ops:
  59.9 1.7 %copy-start = (f32[1,3,16,1024]{3,2,1,0:T(8,128)S(1)}, f32[1,3,16,1024]{3,2,1,0:T(8,128)}, u32[]{:S(2)}) copy-start(f32[1,3,16,1024]{3,2,1,0:T(8,128)} %get-tuple-element.5) | copy-start | bytes 589828

commit v3 on v2

--- a/solution.py
+++ b/solution.py
@@ -92,9 +92,9 @@
     out_ref, flow_ref,
     head, soils, kind, store, cond, cap, face_l, face_r, face_c, diag, dinv, t0, t1, t2, t3,
     water, enter, leave, rainx, flows, pack_out, pack_in, edge_f, edge_i, edges_f, edges_i,
-    stage_f, stage_i, stage_r, rows_out, landed, stats,
-    met_sem, own_sem, load_sem, swap_send, swap_recv, row_send, row_recv, rain_send, rain_recv,
-    col_send, col_recv, land_send, land_recv, sum_send, sum_recv, flow_send, flow_recv, back_send, back_recv,
+    stage_f, stage_i, stage_r, rows_out, landed, stats, gauge, of_kind,
+    met_sem, load_sem, table_sem, own_sem, swap_send, swap_recv, row_send, row_recv, rain_recv,
+    col_send, col_recv, land_send, land_recv, sum_send, sum_recv, out_send, out_recv, out_own,
 ):
     f32 = jnp.float32
     layers, rows, wide = start_ref.shape
@@ -120,15 +120,30 @@
     sec_peers = [lax.rem(sec + k, n_sec) for k in range(1, n_sec)]
     sec_froms = [lax.rem(sec + n_sec - k, n_sec) for k in range(n_sec)]
     gx_peers = [lax.rem(gx + k, n_gx) for k in range(1, n_gx)]
+    swap_size = 2 * rows * (layers * tiles + 1)
+    row_size = 2 * RIM * (layers * tiles + 1)
+    rain_size = steps * (tiles + 1) * RIM
+    land_size = ITERS * (total // 2) * tiles * RIM
+    flow_size = steps * rows * tiles
+    back_size = layers * rows * tiles
+
+    def drain(size, sem):
+        lot = gauge.at[0:size]
+        pltpu.make_async_copy(lot, lot, sem).wait()
+
     everyone = [
         {"sec": mirrored(sec, i, n_sec), "gx": mirrored(gx, j, n_gx)}
         for j in reversed(range(n_gx)) for i in reversed(range(n_sec)) if i + j
     ]
 
     loads = [
-        pltpu.make_async_copy(src, dst, load_sem.at[f])
-        for f, (src, dst) in enumerate(((start_ref, stage_f), (soil_ref, stage_i), (rain_ref, stage_r)))
+        pltpu.make_async_copy(src, dst, load_sem)
+        for src, dst in ((start_ref, stage_f), (soil_ref, stage_i), (rain_ref, stage_r))
     ]
+    tables = [
+        pltpu.make_async_copy(src, of_kind.at[f], table_sem.at[f]) for f, src in enumerate((cond_ref, store_ref))
+    ]
+    loads += tables
     for copy in loads:
         copy.start()
     barrier = pltpu.get_barrier_semaphore()
@@ -184,8 +199,7 @@
     beside = beside | ((lane < RIM) & (here == n_sec - 1)) | ((lane >= LANES - RIM) & (here == 0))
     outside = [beyond] * tiles + [beyond | beside]
 
-    for copy in loads:
-        copy.wait()
+    drain((2 * layers + steps) * rows * wide // LANES, load_sem)
 
     after = lanes_at(lax.rem(here + 1, n_sec), 0)
     before = lanes_at(lax.rem(here + n_sec - 1, n_sec), tiles - 1)
@@ -217,9 +231,9 @@
     for f, (stage, field, edges, edge) in enumerate(parcels):
         for ct in inner:
             swaps[0].append(pltpu.make_async_copy(
-                stage.at[:, :, lanes_at(here, ct)], field.at[layers_of(sec), ct, own], own_sem.at[f, ct]
+                stage.at[:, :, lanes_at(here, ct)], field.at[layers_of(sec), ct, own], own_sem
             ))
-        swaps[0].append(pltpu.make_async_copy(edges.at[here], edge.at[sec, own], own_sem.at[f, tiles]))
+        swaps[0].append(pltpu.make_async_copy(edges.at[here], edge.at[sec, own], own_sem))
     for k, peer in enumerate(sec_peers):
         for f, (stage, field, edges, edge) in enumerate(parcels):
             moves = [
@@ -230,8 +244,8 @@
                 swaps[k + 1].append(pltpu.make_async_remote_copy(
                     src_ref=src,
                     dst_ref=dst,
-                    send_sem=swap_send.at[k, f, m],
-                    recv_sem=swap_recv.at[k, f, m],
+                    send_sem=swap_send,
+                    recv_sem=swap_recv.at[k],
                     device_id={"sec": peer},
                     device_id_type=MESH,
                 ))
@@ -253,7 +267,7 @@
         return pltpu.make_async_remote_copy(
             src_ref=rainx.at[:, :, src],
             dst_ref=rainx.at[:, :, dst],
-            send_sem=rain_send.at[d],
+            send_sem=row_send.at[d],
             recv_sem=rain_recv.at[d],
             device_id={"gx": toward(d)},
             device_id_type=MESH,
@@ -270,8 +284,8 @@
                 copies.append(pltpu.make_async_remote_copy(
                     src_ref=a,
                     dst_ref=b,
-                    send_sem=row_send.at[k, f, d, m],
-                    recv_sem=row_recv.at[k, f, d, m],
+                    send_sem=row_send.at[d],
+                    recv_sem=row_recv.at[k, d],
                     device_id={"gx": toward(d)},
                     device_id_type=MESH,
                 ))
@@ -283,8 +297,7 @@
             rain_copy(d).start()
 
     for k in range(n_sec):
-        for copy in swaps[k]:
-            copy.wait()
+        drain(swap_size, own_sem if k == 0 else swap_recv.at[k - 1])
         for d in (0, 1):
             @pl.when(sends_to(d))
             def _(d=d, k=k):
@@ -295,10 +308,7 @@
         for d in (0, 1):
             @pl.when(sends_to(d))
             def _(d=d):
-                for copy in row_copies(k, d):
-                    copy.wait_send()
-                for copy in row_copies(k, 1 - d):
-                    copy.wait_recv()
+                drain(row_size, row_recv.at[k, 1 - d])
 
     def packed(tile, low):
         outs = nil(ext, LANES)
@@ -313,8 +323,8 @@
         return pltpu.make_async_remote_copy(
             src_ref=pack_out.at[c, d],
             dst_ref=pack_in.at[c, d],
-            send_sem=col_send.at[c, d],
-            recv_sem=col_recv.at[c, d],
+            send_sem=col_send.at[d],
+            recv_sem=col_recv.at[d],
             device_id={"sec": place_of(lax.rem(here + n_sec - 1, n_sec) if d == 0 else lax.rem(here + 1, n_sec))},
             device_id_type=MESH,
         )
@@ -366,13 +376,13 @@
     none = nil(RIM, LANES)
     basis = (t0, t1, t2, t3)
 
-    def back_copies(k, peer):
+    def back_copies(peer):
         return [
             pltpu.make_async_remote_copy(
                 src_ref=head.at[layers_of(peer), ct, own],
                 dst_ref=out_ref.at[:, :, lanes_at(here, ct)],
-                send_sem=back_send.at[k, ct],
-                recv_sem=back_recv.at[k, ct],
+                send_sem=out_send,
+                recv_sem=out_recv,
                 device_id={"sec": peer},
                 device_id_type=MESH,
             )
@@ -393,9 +403,11 @@
     spot = lax.broadcasted_iota(jnp.int32, (ext, LANES), 1)
     of_cond = nil(ext, LANES)
     of_store = nil(ext, LANES)
+    for copy in tables:
+        copy.wait()
     for k in range(kinds):
-        of_cond = jnp.where(spot == k, cond_ref[k], of_cond)
-        of_store = jnp.where(spot == k, store_ref[k], of_store)
+        of_cond = jnp.where(spot == k, of_kind[0, k], of_cond)
+        of_store = jnp.where(spot == k, of_kind[1, k], of_store)
 
     def open_edges(s):
         for edge, field in ((edge_f, head), (edge_i, soils)):
@@ -416,7 +428,6 @@
                 kind[l, ct] = jnp.where(outside[ct], 0.0, a)
                 store[l, ct] = jnp.where(outside[ct], 0.0, b)
 
-    outgoing = []
     for c in range(steps):
         def couple(which, c=c):
             depth = jnp.float32(layers)
@@ -468,29 +479,25 @@
             for d in (0, 1):
                 @pl.when(sends_to(d))
                 def _(d=d):
-                    rain_copy(d).wait_send()
                     rain_copy(1 - d).wait_recv()
         else:
             send_cols(c - 1)
 
         prepare(inner)
         own_flow = pltpu.make_async_copy(
-            flows.at[sec, c], flow_ref.at[0, c, :, pl.ds(pl.multiple_of(here * cols, LANES), cols)], flow_send.at[c, n_sec - 1]
+            flows.at[sec, c], flow_ref.at[0, c, :, pl.ds(pl.multiple_of(here * cols, LANES), cols)], out_own
         )
         own_flow.start()
-        late = [own_flow]
         for k, peer in enumerate(sec_peers):
             copy = pltpu.make_async_remote_copy(
                 src_ref=flows.at[peer, c],
                 dst_ref=flow_ref.at[0, c, :, pl.ds(pl.multiple_of(here * cols, LANES), cols)],
-                send_sem=flow_send.at[c, k],
-                recv_sem=flow_recv.at[c, k],
+                send_sem=out_send,
+                recv_sem=out_recv,
                 device_id={"sec": peer},
                 device_id_type=MESH,
             )
             copy.start()
-            late.append(copy)
-        outgoing += late
 
         if c > 0:
             take_cols(c - 1)
@@ -539,8 +546,8 @@
             return pltpu.make_async_remote_copy(
                 src_ref=rows_out.at[k, d],
                 dst_ref=landed.at[c, k, d],
-                send_sem=land_send.at[c, k, d],
-                recv_sem=land_recv.at[c, k, d],
+                send_sem=land_send.at[d],
+                recv_sem=land_recv.at[c, d],
                 device_id={"gx": toward(d)},
                 device_id_type=MESH,
             )
@@ -607,20 +614,23 @@
         stats[c, mine] = jnp.sum(jnp.where(which == group, flat, 0.0), axis=0, keepdims=True)
         if c == 0:
             pl.semaphore_wait(met_sem, n_sec - 1)
-        sends = []
         for k, peer in enumerate(everyone):
             copy = pltpu.make_async_remote_copy(
                 src_ref=stats.at[c, mine],
                 dst_ref=stats.at[c, mine],
-                send_sem=sum_send.at[c, k],
-                recv_sem=sum_recv.at[c, k],
+                send_sem=sum_send,
+                recv_sem=sum_recv.at[c],
                 device_id=peer,
                 device_id_type=MESH,
             )
             copy.start()
-            sends.append(copy)
-        for copy in sends:
-            copy.wait()
+        drain(len(everyone), sum_recv.at[c])
+        drain(len(everyone), sum_send)
+        if c == 0:
+            for d in (0, 1):
+                @pl.when(sends_to(d))
+                def _(d=d):
+                    drain(n_sec * row_size + rain_size, row_send.at[d])
         summed = stats[c, 0]
         for k in range(1, n_sec * n_gx):
             summed = summed + stats[c, k]
@@ -648,19 +658,16 @@
             for i in range(1, n_sec):
                 peer = sec_peers[i - 1]
                 by_group(1 + peer * layers, 1 + (peer + 1) * layers, layers, update, 0)
-                for copy in back_copies(i - 1, peer):
+                for copy in back_copies(peer):
                     copy.start()
-                    outgoing.append(copy)
             by_group(1 + sec * layers, 1 + (sec + 1) * layers, layers, update, 0)
         else:
             by_group(1, total + 1, layers, update, 0)
             for d in (0, 1):
                 @pl.when(sends_to(d))
                 def _(d=d):
-                    for k in range(ITERS):
-                        land_copy(k, d).wait_send()
-                    for k in range(ITERS):
-                        land_copy(k, 1 - d).wait_recv()
+                    drain(land_size, land_send.at[d])
+                    drain(land_size, land_recv.at[c, 1 - d])
 
             def update_rim(i, carry):
                 for d in (0, 1):
@@ -678,12 +685,13 @@
 
     for ct in inner:
         copy = pltpu.make_async_copy(
-            head.at[layers_of(sec), ct, own], out_ref.at[:, :, lanes_at(here, ct)], back_send.at[n_sec - 1, ct]
+            head.at[layers_of(sec), ct, own], out_ref.at[:, :, lanes_at(here, ct)], out_own
         )
         copy.start()
-        outgoing.append(copy)
-    for copy in outgoing:
-        copy.wait()
+    drain((n_sec - 1) * swap_size, swap_send)
+    drain(flow_size + back_size, out_own)
+    drain((n_sec - 1) * (flow_size + back_size), out_send)
+    drain((n_sec - 1) * (flow_size + back_size), out_recv)
 
 
 def body(n_sec, n_gx, start, soil, conductivity, storage, rain):
@@ -699,15 +707,22 @@
     field = pltpu.VMEM((total + 2, tiles + 1, ext, LANES), f32)
     per_sec = pltpu.VMEM((n_sec, tiles + 1, ext, LANES), f32)
     dma = pltpu.SemaphoreType.DMA
+    longest = max(
+        (2 * layers + steps) * rows * wide // LANES,
+        2 * rows * (layers * tiles + 1) * (n_sec - 1),
+        2 * RIM * (layers * tiles + 1) * n_sec + steps * (tiles + 1) * RIM,
+        ITERS * (total // 2) * tiles * RIM,
+        (n_sec - 1) * (steps + layers) * rows * tiles,
+        n_sec * n_gx,
+    )
     hbm = pl.BlockSpec(memory_space=pl.ANY)
-    smem = pl.BlockSpec(memory_space=pltpu.SMEM)
     return tuple(pl.pallas_call(
         functools.partial(kernel, n_sec, n_gx, steps, conductivity.shape[0]),
         out_shape=(
             jax.ShapeDtypeStruct(start.shape, f32),
             jax.ShapeDtypeStruct((1, steps, rows, wide), f32),
         ),
-        in_specs=[hbm, hbm, smem, smem, hbm],
+        in_specs=[hbm] * 5,
         out_specs=(hbm, hbm),
         scratch_shapes=[field, pltpu.VMEM((total + 2, tiles + 1, ext, LANES), i32)]
         + [field] * 13
@@ -727,25 +742,26 @@
             pltpu.VMEM((ITERS, 2, total // 2, tiles, RIM, LANES), f32),
             pltpu.VMEM((steps - 1, ITERS, 2, total // 2, tiles, RIM, LANES), f32),
             pltpu.VMEM((steps, n_sec * n_gx, 1, LANES), f32),
+            pltpu.VMEM((longest, LANES), f32),
+            pltpu.SMEM((2, conductivity.shape[0]), f32),
             pltpu.SemaphoreType.REGULAR,
-            dma((2, tiles + 1)),
-            dma((3,)),
-            dma((n_sec - 1, 2, tiles + 1)),
-            dma((n_sec - 1, 2, tiles + 1)),
-            dma((n_sec, 2, 2, 2)),
-            dma((n_sec, 2, 2, 2)),
+            dma,
+            dma((2,)),
+            dma,
+            dma,
+            dma((n_sec - 1,)),
+            dma((2,)),
+            dma((n_sec, 2)),
+            dma((2,)),
+            dma((2,)),
             dma((2,)),
             dma((2,)),
             dma((steps - 1, 2)),
-            dma((steps - 1, 2)),
-            dma((steps - 1, ITERS, 2)),
-            dma((steps - 1, ITERS, 2)),
-            dma((steps, n_sec * n_gx)),
-            dma((steps, n_sec * n_gx)),
-            dma((steps, n_sec)),
-            dma((steps, n_sec)),
-            dma((n_sec, tiles)),
-            dma((n_sec, tiles)),
+            dma,
+            dma((steps,)),
+            dma,
+            dma,
+            dma,
         ],
         compiler_params=pltpu.CompilerParams(collective_id=0, has_side_effects=True),
     )(start, soil, conductivity, storage, rain))

time: 62.5 us -> 58.3 us (0.933)
  Pallas kernels: 59.3 us -> 55.2 us
    pallas_call x1, Pallas kernels: 59.3 us -> 55.2 us  [body(): pl.pallas_call(functools.partial(kernel, n_sec, n_gx, steps, conductivity...]
where the time goes in v3:
time: 58.3 us; the launch traced here: 58.2 us
  Pallas kernels  55.2 us (95%)
  local copies, waits for them, and re-layouts  2.39 us (4%)
  between operations  0.65 us (1%)
    pallas_call x1, Pallas kernels, body(): pl.pallas_call(functools.partial(kernel, n_sec, n_gx, steps, conductivity...  55.2 us
    unnamed x4, local copies, waits for them, and re-layouts  2.39 us

profile of v3, /device:TPU:0, one launch (start us, length us, event | category | flops | bytes accessed | tf_op | source)
XLA Modules:
  0.0 58.2 jit_solution(1376814748921343384)
XLA Ops:
  0.6 55.2 %shard_map.68 = (f32[4,16,1024]{2,1,0:T(8,128)}, f32[1,3,16,1024]{3,2,1,0:T(8,128)}) custom-call(f32[4,16,1024]{2,1,0:T(8,128)} %start_ref.1, s32[4,16,1024]{2,1,0:T(8,128)} %soil_ref.1, f32[12]{0:T(128)} %cond_ref.1, f32[12]{0:T(128)} %store_ref.1, f32[3,16,1024]{2,1,0:T(8,128)} %rain_ref.1), custom_call_target="tpu_custom_call" | custom-call | tf_op jit(solution)/shard_map/pallas_call | solution.py:719
  55.8 0.0 copy-start
  55.8 1.7 %copy.9 = f32[4,16,1024]{2,1,0:T(8,128)} copy(f32[4,16,1024]{2,1,0:T(8,128)} %get-tuple-element.4) | data formatting | bytes 524288
  57.5 0.0 copy-done
  57.5 0.7 %copy.10 = f32[1,3,16,1024]{3,2,1,0:T(8,128)} copy(f32[1,3,16,1024]{3,2,1,0:T(8,128)S(1)} %copy-done) | data formatting | bytes 393216
Async XLA Ops:
  55.8 1.7 %copy-start = (f32[1,3,16,1024]{3,2,1,0:T(8,128)S(1)}, f32[1,3,16,1024]{3,2,1,0:T(8,128)}, u32[]{:S(2)}) copy-start(f32[1,3,16,1024]{3,2,1,0:T(8,128)} %get-tuple-element.5) | copy-start | bytes 589828

commit v4 on v3

--- a/solution.py
+++ b/solution.py
@@ -90,7 +90,7 @@
     n_sec, n_gx, steps, kinds,
     start_ref, soil_ref, cond_ref, store_ref, rain_ref,
     out_ref, flow_ref,
-    head, soils, kind, store, cond, cap, face_l, face_r, face_c, diag, dinv, t0, t1, t2, t3,
+    head, soils, kind, store, cond, cap, face_l, face_r, face_c, diag, dinv, t,
     water, enter, leave, rainx, flows, pack_out, pack_in, edge_f, edge_i, edges_f, edges_i,
     stage_f, stage_i, stage_r, rows_out, landed, stats, gauge, of_kind,
     met_sem, load_sem, table_sem, own_sem, swap_send, swap_recv, row_send, row_recv, rain_recv,
@@ -131,6 +131,7 @@
         lot = gauge.at[0:size]
         pltpu.make_async_copy(lot, lot, sem).wait()
 
+    parts_of = ((0, ITERS - 1), (ITERS - 1, ITERS))
     everyone = [
         {"sec": mirrored(sec, i, n_sec), "gx": mirrored(gx, j, n_gx)}
         for j in reversed(range(n_gx)) for i in reversed(range(n_sec)) if i + j
@@ -155,12 +156,13 @@
     def nil(*shape, dtype=f32):
         return jnp.zeros(shape, dtype)
 
-    for ref in (head, cond, t0, t1, t2, t3, face_l):
+    basis = [t.at[k] for k in range(ITERS)]
+    for ref in (head, cond, face_l, *basis):
         ref[0] = nil(tiles + 1, ext, LANES)
         ref[total + 1] = nil(tiles + 1, ext, LANES)
 
     def hem(l, carry):
-        for ref in (t0, t1, t2, t3, face_r):
+        for ref in (face_r, *basis):
             ref[l, :, 0:RIM] = nil(tiles + 1, RIM, LANES)
             ref[l, :, ext - RIM:ext] = nil(tiles + 1, RIM, LANES)
         return carry
@@ -188,7 +190,7 @@
         @pl.when(here == n_sec - 1 if d == 0 else here == 0)
         def _(d=d):
             for c in range(steps - 1):
-                pack_in[c, d] = nil(ext, LANES)
+                pack_in[c, d] = nil(ITERS, ext, LANES)
 
     lane = lax.broadcasted_iota(jnp.int32, (ext, LANES), 1)
     lane_w = lax.broadcasted_iota(jnp.int32, (rows + RIM, LANES), 1)
@@ -310,49 +312,75 @@
             def _(d=d):
                 drain(row_size, row_recv.at[k, 1 - d])
 
-    def packed(tile, low):
+    def packed(k, tile, low):
         outs = nil(ext, LANES)
         for l in range(total):
             shift = (RIM * l if low else RIM * l + RIM) % LANES
-            piece = head[1 + l, tile]
+            piece = t[k, 1 + l, tile]
             moved = pltpu.roll(piece, shift, 1) if shift else piece
             outs = jnp.where(lane // RIM == l, moved, outs)
         return outs
 
-    def col_copy(c, d):
+    def col_copy(c, d, part):
+        low, high = parts_of[part]
         return pltpu.make_async_remote_copy(
-            src_ref=pack_out.at[c, d],
-            dst_ref=pack_in.at[c, d],
+            src_ref=pack_out.at[d, low:high],
+            dst_ref=pack_in.at[c, d, low:high],
             send_sem=col_send.at[d],
-            recv_sem=col_recv.at[d],
+            recv_sem=col_recv.at[c, d, part],
             device_id={"sec": place_of(lax.rem(here + n_sec - 1, n_sec) if d == 0 else lax.rem(here + 1, n_sec))},
             device_id_type=MESH,
         )
 
-    def send_cols(c):
+    def beside_to(d):
+        return here > 0 if d == 0 else here < n_sec - 1
+
+    def settle(c, part):
+        low, high = parts_of[part]
         for d in (0, 1):
-            @pl.when(here > 0 if d == 0 else here < n_sec - 1)
+            @pl.when(sends_to(d))
             def _(d=d):
-                pack_out[c, d] = packed(0 if d == 0 else tiles - 1, d == 0)
-                col_copy(c, d).start()
-
-    def take_cols(c):
-        @pl.when(here > 0)
-        def _():
-            col_copy(c, 0).wait_send()
-            col_copy(c, 1).wait_recv()
-
-        @pl.when(here < n_sec - 1)
-        def _():
-            col_copy(c, 1).wait_send()
-            col_copy(c, 0).wait_recv()
-
-        right, left = pack_in[c, 0], pack_in[c, 1]
-        for l in range(total):
-            a, b = (-RIM * l) % LANES, (LANES - RIM - RIM * l) % LANES
-            ra = pltpu.roll(right, a, 1) if a else right
-            rb = pltpu.roll(left, b, 1) if b else left
-            head[1 + l, tiles] = jnp.where(lane < RIM, ra, jnp.where(lane >= LANES - RIM, rb, 0.0))
+                drain((high - low) * land_size // ITERS, land_recv.at[c, 1 - d, part])
+
+        def place(i, carry):
+            for d in (0, 1):
+                first_row = RIM + rows + 1 if d == 0 else RIM - LOW
+                for k in range(low, high):
+                    for ct in inner:
+                        for j in (0, 1):
+                            t[k, 1 + 2 * i + j, ct, first_row:first_row + LOW] = landed[
+                                c, k, d, i, ct, j * LOW:j * LOW + LOW
+                            ]
+            return carry
+
+        by_group(0, total // 2, 2, place, 0)
+        for d in (0, 1):
+            @pl.when(beside_to(d))
+            def _(d=d):
+                def each(k, carry):
+                    pack_out[d, k] = packed(k, 0 if d == 0 else tiles - 1, d == 0)
+                    return carry
+
+                lax.fori_loop(low, high, each, 0)
+                col_copy(c, d, part).start()
+
+    def take_cols(c, part):
+        low, high = parts_of[part]
+        for d in (0, 1):
+            @pl.when(beside_to(d))
+            def _(d=d):
+                col_copy(c, 1 - d, part).wait_recv()
+
+        def each(k, carry):
+            right, left = pack_in[c, 0, k], pack_in[c, 1, k]
+            for l in range(total):
+                a, b = (-RIM * l) % LANES, (LANES - RIM - RIM * l) % LANES
+                ra = pltpu.roll(right, a, 1) if a else right
+                rb = pltpu.roll(left, b, 1) if b else left
+                t[k, 1 + l, tiles] = jnp.where(lane < RIM, ra, jnp.where(lane >= LANES - RIM, rb, 0.0))
+            return carry
+
+        lax.fori_loop(low, high, each, 0)
 
     def right_of(v, at):
         moved = [pltpu.roll(a, LANES - 1, 1) for a in v]
@@ -374,7 +402,6 @@
         return out
 
     none = nil(RIM, LANES)
-    basis = (t0, t1, t2, t3)
 
     def back_copies(peer):
         return [
@@ -446,28 +473,13 @@
                     entering = slopes[s] * entering + 0.5 * cond[(s + 1) * layers, ct]
                     leave[s, ct] = entering
 
-        def faces(which, l, carry):
-            for ct in which:
-                k = cond[l, ct, work]
-                face_l[l, ct, work] = harmonic(k, cond[l + 1, ct, work])
-                face_r[l, ct, work] = harmonic(k, cond[l, ct, under])
-            return carry
-
-        def faces_across(l, carry):
+        def faces(l, carry):
             k = [cond[l, ct, work] for ct in everywhere]
             for ct, other in zip(everywhere, right_of(k, lane_w)):
+                face_l[l, ct, work] = harmonic(k[ct], cond[l + 1, ct, work])
+                face_r[l, ct, work] = harmonic(k[ct], cond[l, ct, under])
                 face_c[l, ct, work] = harmonic(k[ct], other)
             return carry
-
-        def prepare(which, c=c):
-            if c > 0:
-                def each(s, carry):
-                    soil(which, s)
-                    return carry
-
-                lax.fori_loop(0, n_sec, each, 0)
-            couple(which)
-            by_group(1, total + 1, layers, functools.partial(faces, which), 0)
 
         if c == 0:
             for k in range(n_sec):
@@ -481,9 +493,12 @@
                 def _(d=d):
                     rain_copy(1 - d).wait_recv()
         else:
-            send_cols(c - 1)
-
-        prepare(inner)
+            def each(s, carry):
+                soil(everywhere, s)
+                return carry
+
+            lax.fori_loop(0, n_sec, each, 0)
+        couple(everywhere)
         own_flow = pltpu.make_async_copy(
             flows.at[sec, c], flow_ref.at[0, c, :, pl.ds(pl.multiple_of(here * cols, LANES), cols)], out_own
         )
@@ -499,10 +514,7 @@
             )
             copy.start()
 
-        if c > 0:
-            take_cols(c - 1)
-        prepare([tiles])
-        by_group(1, total + 1, layers, faces_across, 0)
+        by_group(1, total + 1, layers, faces, 0)
 
         def rows_of(k, l, m):
             if c + 1 < steps:
@@ -535,7 +547,7 @@
                     z = res * inverse
                     diag[l, ct, work] = whole
                     dinv[l, ct, work] = 2.0 * inverse
-                    t0[l, ct, work] = z
+                    basis[0][l, ct, work] = z
                     if ct < tiles:
                         acc = acc + own_of(res * z)
             for j in range(0, layers, 2):
@@ -547,7 +559,7 @@
                 src_ref=rows_out.at[k, d],
                 dst_ref=landed.at[c, k, d],
                 send_sem=land_send.at[d],
-                recv_sem=land_recv.at[c, d],
+                recv_sem=land_recv.at[c, d, 0 if k < ITERS - 1 else 1],
                 device_id={"gx": toward(d)},
                 device_id_type=MESH,
             )
@@ -564,16 +576,16 @@
         h = []
         for k in range(ITERS - 1):
             def apply(i, acc, k=k):
-                t = basis[k]
+                v_of = basis[k]
                 for j in range(layers):
                     l = 1 + i * layers + j
-                    v = [t[l, ct, work] for ct in everywhere]
+                    v = [v_of[l, ct, work] for ct in everywhere]
                     fc = [face_c[l, ct, work] for ct in everywhere]
                     aside = right_of(v, lane_w)
                     back = left_of([a * b for a, b in zip(fc, v)], lane_w)
                     for ct in everywhere:
-                        near = face_l[l - 1, ct, work] * t[l - 1, ct, work] + face_l[l, ct, work] * t[l + 1, ct, work]
-                        near = near + face_r[l, ct, work] * t[l, ct, under] + face_r[l, ct, above] * t[l, ct, above]
+                        near = face_l[l - 1, ct, work] * v_of[l - 1, ct, work] + face_l[l, ct, work] * v_of[l + 1, ct, work]
+                        near = near + face_r[l, ct, work] * v_of[l, ct, under] + face_r[l, ct, above] * v_of[l, ct, above]
                         near = near + (fc[ct] * aside[ct] + back[ct])
                         new = dinv[l, ct, work] * near
                         new = 0.5 * new if k == 0 else new - basis[k - 1][l, ct, work]
@@ -590,12 +602,12 @@
             send_land(k + 1)
 
         def last(l, acc):
-            t = basis[ITERS - 1]
-            v = [t[l, ct, own] for ct in everywhere]
+            v_of = basis[ITERS - 1]
+            v = [v_of[l, ct, own] for ct in everywhere]
             aside = right_of(v, lane_o)
             for ct in inner:
-                near = face_l[l, ct, own] * t[l + 1, ct, own] + face_c[l, ct, own] * aside[ct]
-                near = v[ct] * (near + face_r[l, ct, own] * t[l, ct, RIM + 1:RIM + rows + 1])
+                near = face_l[l, ct, own] * v_of[l + 1, ct, own] + face_c[l, ct, own] * aside[ct]
+                near = v[ct] * (near + face_r[l, ct, own] * v_of[l, ct, RIM + 1:RIM + rows + 1])
                 for i in range(0, rows, RIM):
                     acc = acc + near[i:i + RIM]
             return acc
@@ -624,6 +636,19 @@
                 device_id_type=MESH,
             )
             copy.start()
+        if c + 1 < steps:
+            settle(c, 0)
+            settle(c, 1)
+            take_cols(c, 0)
+            take_cols(c, 1)
+            for d in (0, 1):
+                @pl.when(sends_to(d))
+                def _(d=d):
+                    drain(land_size, land_send.at[d])
+
+                @pl.when(beside_to(d))
+                def _(d=d):
+                    drain(ITERS * ext, col_send.at[d])
         drain(len(everyone), sum_recv.at[c])
         drain(len(everyone), sum_send)
         if c == 0:
@@ -639,49 +664,26 @@
             for k in range(2 * ITERS)
         ]
         x = coefficients(parts[:ITERS], parts[ITERS:])
-        x = [jnp.broadcast_to(v, (rows, LANES)) for v in x]
-
-        def update(l, carry):
-            for ct in inner:
-                v = head[l, ct, own]
+        x = [jnp.broadcast_to(v, (ext, LANES)) for v in x]
+
+        def update(which, at_rows, count, l, carry):
+            for ct in which:
+                v = head[l, ct, at_rows]
                 for k in range(ITERS):
-                    v = v + x[k] * basis[k][l, ct, own]
-                head[l, ct, own] = v
-                if c + 1 < steps:
-                    v = head[l, ct, RIM + rows:RIM + rows + 1]
-                    for k in range(ITERS):
-                        v = v + x[k][0:1] * basis[k][l, ct, RIM + rows:RIM + rows + 1]
-                    head[l, ct, RIM + rows:RIM + rows + 1] = v
+                    v = v + x[k][0:count] * t[k, l, ct, at_rows]
+                head[l, ct, at_rows] = v
             return carry
 
         if c + 1 == steps:
+            final = functools.partial(update, inner, own, rows)
             for i in range(1, n_sec):
                 peer = sec_peers[i - 1]
-                by_group(1 + peer * layers, 1 + (peer + 1) * layers, layers, update, 0)
+                by_group(1 + peer * layers, 1 + (peer + 1) * layers, layers, final, 0)
                 for copy in back_copies(peer):
                     copy.start()
-            by_group(1 + sec * layers, 1 + (sec + 1) * layers, layers, update, 0)
+            by_group(1 + sec * layers, 1 + (sec + 1) * layers, layers, final, 0)
         else:
-            by_group(1, total + 1, layers, update, 0)
-            for d in (0, 1):
-                @pl.when(sends_to(d))
-                def _(d=d):
-                    drain(land_size, land_send.at[d])
-                    drain(land_size, land_recv.at[c, 1 - d])
-
-            def update_rim(i, carry):
-                for d in (0, 1):
-                    first_row = RIM + rows + 1 if d == 0 else RIM - LOW
-                    at_rows = slice(first_row, first_row + LOW)
-                    for ct in inner:
-                        for j in (0, 1):
-                            v = head[1 + 2 * i + j, ct, at_rows]
-                            for k in range(ITERS):
-                                v = v + x[k][0:LOW] * landed[c, k, d, i, ct, j * LOW:j * LOW + LOW]
-                            head[1 + 2 * i + j, ct, at_rows] = v
-                return carry
-
-            by_group(0, total // 2, 2, update_rim, 0)
+            by_group(1, total + 1, layers, functools.partial(update, everywhere, slice(0, ext), ext), 0)
 
     for ct in inner:
         copy = pltpu.make_async_copy(
@@ -712,6 +714,7 @@
         2 * rows * (layers * tiles + 1) * (n_sec - 1),
         2 * RIM * (layers * tiles + 1) * n_sec + steps * (tiles + 1) * RIM,
         ITERS * (total // 2) * tiles * RIM,
+        ITERS * ext,
         (n_sec - 1) * (steps + layers) * rows * tiles,
         n_sec * n_gx,
     )
@@ -725,13 +728,14 @@
         in_specs=[hbm] * 5,
         out_specs=(hbm, hbm),
         scratch_shapes=[field, pltpu.VMEM((total + 2, tiles + 1, ext, LANES), i32)]
-        + [field] * 13
+        + [field] * 9
+        + [pltpu.VMEM((ITERS, total + 2, tiles + 1, ext, LANES), f32)]
         + [per_sec] * 3
         + [
             pltpu.VMEM((steps, tiles + 1, ext, LANES), f32),
             pltpu.VMEM((n_sec, steps, rows, cols), f32),
-            pltpu.VMEM((steps - 1, 2, ext, LANES), f32),
-            pltpu.VMEM((steps - 1, 2, ext, LANES), f32),
+            pltpu.VMEM((2, ITERS, ext, LANES), f32),
+            pltpu.VMEM((steps - 1, 2, ITERS, ext, LANES), f32),
             pltpu.VMEM((n_sec, ext, LANES), f32),
             pltpu.VMEM((n_sec, ext, LANES), i32),
             pltpu.VMEM((n_sec, rows, LANES), f32),
@@ -754,9 +758,9 @@
             dma((n_sec, 2)),
             dma((2,)),
             dma((2,)),
+            dma((steps - 1, 2, 2)),
             dma((2,)),
-            dma((2,)),
-            dma((steps - 1, 2)),
+            dma((steps - 1, 2, 2)),
             dma,
             dma((steps,)),
             dma,

time: 58.3 us -> 55.4 us (0.950)
  Pallas kernels: 55.2 us -> 52.2 us
    pallas_call x1, Pallas kernels: 55.2 us -> 52.2 us  [body(): pl.pallas_call(functools.partial(kernel, n_sec, n_gx, steps, conductivity...]
where the time goes in v4:
time: 55.4 us; the launch traced here: 55.2 us
  Pallas kernels  52.2 us (94%)
  local copies, waits for them, and re-layouts  2.39 us (4%)
  between operations  0.65 us (1%)
    pallas_call x1, Pallas kernels, body(): pl.pallas_call(functools.partial(kernel, n_sec, n_gx, steps, conductivity...  52.2 us
    unnamed x4, local copies, waits for them, and re-layouts  2.39 us

profile of v4, /device:TPU:0, one launch (start us, length us, event | category | flops | bytes accessed | tf_op | source)
XLA Modules:
  0.0 55.2 jit_solution(5590921608518517123)
XLA Ops:
  0.6 52.2 %shard_map.68 = (f32[4,16,1024]{2,1,0:T(8,128)}, f32[1,3,16,1024]{3,2,1,0:T(8,128)}) custom-call(f32[4,16,1024]{2,1,0:T(8,128)} %start_ref.1, s32[4,16,1024]{2,1,0:T(8,128)} %soil_ref.1, f32[12]{0:T(128)} %cond_ref.1, f32[12]{0:T(128)} %store_ref.1, f32[3,16,1024]{2,1,0:T(8,128)} %rain_ref.1), custom_call_target="tpu_custom_call" | custom-call | tf_op jit(solution)/shard_map/pallas_call | solution.py:722
  52.8 0.0 copy-start
  52.8 1.7 %copy.9 = f32[4,16,1024]{2,1,0:T(8,128)} copy(f32[4,16,1024]{2,1,0:T(8,128)} %get-tuple-element.4) | data formatting | bytes 524288
  54.5 0.0 copy-done
  54.5 0.7 %copy.10 = f32[1,3,16,1024]{3,2,1,0:T(8,128)} copy(f32[1,3,16,1024]{3,2,1,0:T(8,128)S(1)} %copy-done) | data formatting | bytes 393216
Async XLA Ops:
  52.8 1.7 %copy-start = (f32[1,3,16,1024]{3,2,1,0:T(8,128)S(1)}, f32[1,3,16,1024]{3,2,1,0:T(8,128)}, u32[]{:S(2)}) copy-start(f32[1,3,16,1024]{3,2,1,0:T(8,128)} %get-tuple-element.5) | copy-start | bytes 589828

commit v5 on v4

--- a/solution.py
+++ b/solution.py
@@ -13,6 +13,7 @@
 LANES = 128
 ITERS = 4
 LOW = RIM // 2
+SHIPPED = (((0, 0), (1, 1)), ((2, 0),), ((3, 0),))
 
 
 def by_group(low, high, each, body, carry):
@@ -91,7 +92,7 @@
     start_ref, soil_ref, cond_ref, store_ref, rain_ref,
     out_ref, flow_ref,
     head, soils, kind, store, cond, cap, face_l, face_r, face_c, diag, dinv, t,
-    water, enter, leave, rainx, flows, pack_out, pack_in, edge_f, edge_i, edges_f, edges_i,
+    water, enter, leave, rainx, flows, pack_out, pack_in, side, edge_f, edge_i, edges_f, edges_i,
     stage_f, stage_i, stage_r, rows_out, landed, stats, gauge, of_kind,
     met_sem, load_sem, table_sem, own_sem, swap_send, swap_recv, row_send, row_recv, rain_recv,
     col_send, col_recv, land_send, land_recv, sum_send, sum_recv, out_send, out_recv, out_own,
@@ -123,7 +124,7 @@
     swap_size = 2 * rows * (layers * tiles + 1)
     row_size = 2 * RIM * (layers * tiles + 1)
     rain_size = steps * (tiles + 1) * RIM
-    land_size = ITERS * (total // 2) * tiles * RIM
+    land_size = (total // 2) * tiles * RIM
     flow_size = steps * rows * tiles
     back_size = layers * rows * tiles
 
@@ -184,7 +185,7 @@
             edge_f[:, rim] = nil(n_sec, RIM, LANES)
             edge_i[:, rim] = nil(n_sec, RIM, LANES, dtype=jnp.int32)
             for c in range(steps - 1):
-                for k in range(ITERS):
+                for k in range(len(SHIPPED)):
                     landed[c, k, d] = nil(total // 2, tiles, RIM, LANES)
 
         @pl.when(here == n_sec - 1 if d == 0 else here == 0)
@@ -312,11 +313,11 @@
             def _(d=d):
                 drain(row_size, row_recv.at[k, 1 - d])
 
-    def packed(k, tile, low):
+    def packed(field, tile, low):
         outs = nil(ext, LANES)
         for l in range(total):
             shift = (RIM * l if low else RIM * l + RIM) % LANES
-            piece = t[k, 1 + l, tile]
+            piece = field[1 + l, tile]
             moved = pltpu.roll(piece, shift, 1) if shift else piece
             outs = jnp.where(lane // RIM == l, moved, outs)
         return outs
@@ -335,22 +336,31 @@
     def beside_to(d):
         return here > 0 if d == 0 else here < n_sec - 1
 
+    def rows_for(k, d, landing):
+        if d == 0:
+            start = RIM + LOW - k + (rows if landing else 0)
+        else:
+            start = RIM - LOW + (0 if landing else rows)
+        return slice(start, start + k + 1)
+
     def settle(c, part):
         low, high = parts_of[part]
+        lots = [p for p, slots in enumerate(SHIPPED) if low <= slots[0][0] < high]
         for d in (0, 1):
             @pl.when(sends_to(d))
             def _(d=d):
-                drain((high - low) * land_size // ITERS, land_recv.at[c, 1 - d, part])
+                for p in lots:
+                    drain(land_size, land_recv.at[c, 1 - d, p])
 
         def place(i, carry):
             for d in (0, 1):
-                first_row = RIM + rows + 1 if d == 0 else RIM - LOW
-                for k in range(low, high):
-                    for ct in inner:
-                        for j in (0, 1):
-                            t[k, 1 + 2 * i + j, ct, first_row:first_row + LOW] = landed[
-                                c, k, d, i, ct, j * LOW:j * LOW + LOW
-                            ]
+                for p in lots:
+                    for k, spot in SHIPPED[p]:
+                        for ct in inner:
+                            for j in (0, 1):
+                                t[k, 1 + 2 * i + j, ct, rows_for(k, d, True)] = landed[
+                                    c, p, d, i, ct, j * LOW + spot:j * LOW + spot + k + 1
+                                ]
             return carry
 
         by_group(0, total // 2, 2, place, 0)
@@ -358,29 +368,33 @@
             @pl.when(beside_to(d))
             def _(d=d):
                 def each(k, carry):
-                    pack_out[d, k] = packed(k, 0 if d == 0 else tiles - 1, d == 0)
+                    pack_out[d, k] = packed(t.at[k], 0 if d == 0 else tiles - 1, d == 0)
                     return carry
 
                 lax.fori_loop(low, high, each, 0)
                 col_copy(c, d, part).start()
 
-    def take_cols(c, part):
-        low, high = parts_of[part]
+    def take_cols(c):
         for d in (0, 1):
             @pl.when(beside_to(d))
             def _(d=d):
-                col_copy(c, 1 - d, part).wait_recv()
-
-        def each(k, carry):
-            right, left = pack_in[c, 0, k], pack_in[c, 1, k]
-            for l in range(total):
-                a, b = (-RIM * l) % LANES, (LANES - RIM - RIM * l) % LANES
-                ra = pltpu.roll(right, a, 1) if a else right
-                rb = pltpu.roll(left, b, 1) if b else left
-                t[k, 1 + l, tiles] = jnp.where(lane < RIM, ra, jnp.where(lane >= LANES - RIM, rb, 0.0))
-            return carry
-
-        lax.fori_loop(low, high, each, 0)
+                for part in range(len(parts_of)):
+                    col_copy(c, 1 - d, part).wait_recv()
+
+    def side_heads(c, x):
+        sides = []
+        for d in (0, 1):
+            v = side[d]
+            for k in range(ITERS):
+                v = v + x[k] * pack_in[c, d, k]
+            side[d] = v
+            sides.append(v)
+        right, left = sides
+        for l in range(total):
+            a, b = (-RIM * l) % LANES, (LANES - RIM - RIM * l) % LANES
+            ra = pltpu.roll(right, a, 1) if a else right
+            rb = pltpu.roll(left, b, 1) if b else left
+            head[1 + l, tiles] = jnp.where(lane < RIM, ra, jnp.where(lane >= LANES - RIM, rb, 0.0))
 
     def right_of(v, at):
         moved = [pltpu.roll(a, LANES - 1, 1) for a in v]
@@ -516,14 +530,17 @@
 
         by_group(1, total + 1, layers, faces, 0)
 
-        def rows_of(k, l, m):
+        def rows_of(k, l):
             if c + 1 < steps:
                 i = (l - 1) // 2
+                p = next(p for p, slots in enumerate(SHIPPED) if k in dict(slots))
+                spot = dict(SHIPPED[p])[k]
                 for ct in inner:
                     for j in (0, 1):
-                        put = slice(j * LOW, j * LOW + LOW)
-                        rows_out[k, 0, i, ct, put] = basis[k][l + j, ct, RIM + 1:RIM + 1 + LOW]
-                        rows_out[k, 1, i, ct, put] = basis[k][l + j, ct, RIM + rows - LOW:RIM + rows]
+                        for d in (0, 1):
+                            rows_out[p, d, i, ct, j * LOW + spot:j * LOW + spot + k + 1] = basis[k][
+                                l + j, ct, rows_for(k, d, False)
+                            ]
 
         def first(s, acc):
             for j in range(layers):
@@ -551,25 +568,26 @@
                     if ct < tiles:
                         acc = acc + own_of(res * z)
             for j in range(0, layers, 2):
-                rows_of(0, 1 + s * layers + j, s)
+                rows_of(0, 1 + s * layers + j)
             return acc
 
-        def land_copy(k, d, c=c):
+        def land_copy(p, d, c=c):
             return pltpu.make_async_remote_copy(
-                src_ref=rows_out.at[k, d],
-                dst_ref=landed.at[c, k, d],
+                src_ref=rows_out.at[p, d],
+                dst_ref=landed.at[c, p, d],
                 send_sem=land_send.at[d],
-                recv_sem=land_recv.at[c, d, 0 if k < ITERS - 1 else 1],
+                recv_sem=land_recv.at[c, d, p],
                 device_id={"gx": toward(d)},
                 device_id_type=MESH,
             )
 
         def send_land(k):
-            if c + 1 < steps:
-                for d in (0, 1):
-                    @pl.when(sends_to(d))
-                    def _(d=d):
-                        land_copy(k, d).start()
+            for p, slots in enumerate(SHIPPED):
+                if c + 1 < steps and slots[-1][0] == k:
+                    for d in (0, 1):
+                        @pl.when(sends_to(d))
+                        def _(d=d, p=p):
+                            land_copy(p, d).start()
 
         g = [lax.fori_loop(0, n_sec, first, none)]
         send_land(0)
@@ -593,7 +611,7 @@
                         if ct < tiles:
                             acc = (acc[0] + own_of(v[ct] * near), acc[1] + own_of(diag[l, ct, work] * new * new))
                 for j in range(0, layers, 2):
-                    rows_of(k + 1, 1 + i * layers + j, i)
+                    rows_of(k + 1, 1 + i * layers + j)
                 return acc
 
             ah, ag = lax.fori_loop(0, n_sec, apply, (none, none))
@@ -638,13 +656,15 @@
             copy.start()
         if c + 1 < steps:
             settle(c, 0)
+            if c == 0:
+                side[0] = packed(head, tiles, True)
+                side[1] = packed(head, tiles, False)
             settle(c, 1)
-            take_cols(c, 0)
-            take_cols(c, 1)
+            take_cols(c)
             for d in (0, 1):
                 @pl.when(sends_to(d))
                 def _(d=d):
-                    drain(land_size, land_send.at[d])
+                    drain(len(SHIPPED) * land_size, land_send.at[d])
 
                 @pl.when(beside_to(d))
                 def _(d=d):
@@ -683,7 +703,8 @@
                     copy.start()
             by_group(1 + sec * layers, 1 + (sec + 1) * layers, layers, final, 0)
         else:
-            by_group(1, total + 1, layers, functools.partial(update, everywhere, slice(0, ext), ext), 0)
+            by_group(1, total + 1, layers, functools.partial(update, inner, slice(0, ext), ext), 0)
+            side_heads(c, x)
 
     for ct in inner:
         copy = pltpu.make_async_copy(
@@ -696,6 +717,20 @@
     drain((n_sec - 1) * (flow_size + back_size), out_recv)
 
 
+def hand_over(*refs):
+    a, b, out_a, out_b, hold_a, hold_b, sem = refs
+    trips = ((a, hold_a, out_a), (b, hold_b, out_b))
+    come = [pltpu.make_async_copy(src, hold, sem.at[0, i]) for i, (src, hold, _) in enumerate(trips)]
+    go = [pltpu.make_async_copy(hold, dst, sem.at[1, i]) for i, (_, hold, dst) in enumerate(trips)]
+    for copy in come:
+        copy.start()
+    for i in range(2):
+        come[i].wait()
+        go[i].start()
+    for copy in go:
+        copy.wait()
+
+
 def body(n_sec, n_gx, start, soil, conductivity, storage, rain):
     layers, rows, wide = start.shape
     steps = rain.shape[0]
@@ -703,6 +738,7 @@
     tiles = cols // LANES
     total = layers * n_sec
     assert total * RIM <= LANES and cols % LANES == 0 and rows % RIM == 0 and n_sec == 4
+    assert ITERS == LOW and sum(len(slots) for slots in SHIPPED) == ITERS
     assert layers * 2 * RIM <= LANES and layers % 2 == 0 and n_gx & (n_gx - 1) == 0
     ext = rows + 2 * RIM
     f32, i32 = jnp.float32, jnp.int32
@@ -713,13 +749,13 @@
         (2 * layers + steps) * rows * wide // LANES,
         2 * rows * (layers * tiles + 1) * (n_sec - 1),
         2 * RIM * (layers * tiles + 1) * n_sec + steps * (tiles + 1) * RIM,
-        ITERS * (total // 2) * tiles * RIM,
+        len(SHIPPED) * (total // 2) * tiles * RIM,
         ITERS * ext,
         (n_sec - 1) * (steps + layers) * rows * tiles,
         n_sec * n_gx,
     )
     hbm = pl.BlockSpec(memory_space=pl.ANY)
-    return tuple(pl.pallas_call(
+    made = pl.pallas_call(
         functools.partial(kernel, n_sec, n_gx, steps, conductivity.shape[0]),
         out_shape=(
             jax.ShapeDtypeStruct(start.shape, f32),
@@ -736,6 +772,7 @@
             pltpu.VMEM((n_sec, steps, rows, cols), f32),
             pltpu.VMEM((2, ITERS, ext, LANES), f32),
             pltpu.VMEM((steps - 1, 2, ITERS, ext, LANES), f32),
+            pltpu.VMEM((2, ext, LANES), f32),
             pltpu.VMEM((n_sec, ext, LANES), f32),
             pltpu.VMEM((n_sec, ext, LANES), i32),
             pltpu.VMEM((n_sec, rows, LANES), f32),
@@ -743,8 +780,8 @@
             pltpu.VMEM(start.shape, f32),
             pltpu.VMEM(start.shape, i32),
             pltpu.VMEM(rain.shape, f32),
-            pltpu.VMEM((ITERS, 2, total // 2, tiles, RIM, LANES), f32),
-            pltpu.VMEM((steps - 1, ITERS, 2, total // 2, tiles, RIM, LANES), f32),
+            pltpu.VMEM((len(SHIPPED), 2, total // 2, tiles, RIM, LANES), f32),
+            pltpu.VMEM((steps - 1, len(SHIPPED), 2, total // 2, tiles, RIM, LANES), f32),
             pltpu.VMEM((steps, n_sec * n_gx, 1, LANES), f32),
             pltpu.VMEM((longest, LANES), f32),
             pltpu.SMEM((2, conductivity.shape[0]), f32),
@@ -760,7 +797,7 @@
             dma((2,)),
             dma((steps - 1, 2, 2)),
             dma((2,)),
-            dma((steps - 1, 2, 2)),
+            dma((steps - 1, 2, len(SHIPPED))),
             dma,
             dma((steps,)),
             dma,
@@ -768,7 +805,14 @@
             dma,
         ],
         compiler_params=pltpu.CompilerParams(collective_id=0, has_side_effects=True),
-    )(start, soil, conductivity, storage, rain))
+    )(start, soil, conductivity, storage, rain)
+    return tuple(pl.pallas_call(
+        hand_over,
+        out_shape=tuple(jax.ShapeDtypeStruct(a.shape, a.dtype) for a in made),
+        in_specs=[hbm] * 2,
+        out_specs=(hbm,) * 2,
+        scratch_shapes=[pltpu.VMEM(a.shape, a.dtype) for a in made] + [dma((2, 2))],
+    )(*made))
 
 
 def solution(mesh):

time: 55.4 us -> 53.8 us (0.971)
  local copies, waits for them, and re-layouts: 2.39 us -> 0 us
  Pallas kernels: 52.2 us -> 53 us
    unnamed x4 -> x0, local copies, waits for them, and re-layouts: 2.39 us -> none
    pallas_call x0 -> x1, Pallas kernels: none -> 1.75 us  [body(): pl.pallas_call(hand_over, out_shape=tuple((jax.ShapeDtypeStruct(a.shape,...]
    pallas_call x1, Pallas kernels: 52.2 us -> 51.2 us  [body(): pl.pallas_call(functools.partial(kernel, n_sec, n_gx, steps, conductivity...]
where the time goes in v5:
time: 53.8 us; the launch traced here: 53.6 us
  Pallas kernels  53 us (99%)
  between operations  0.64 us (1%)
    pallas_call x1, Pallas kernels, body(): pl.pallas_call(functools.partial(kernel, n_sec, n_gx, steps, conductivity...  51.2 us
    pallas_call x1, Pallas kernels, body(): pl.pallas_call(hand_over, out_shape=tuple((jax.ShapeDtypeStruct(a.shape,...  1.75 us

profile of v5, /device:TPU:0, one launch (start us, length us, event | category | flops | bytes accessed | tf_op | source)
XLA Modules:
  0.0 53.6 jit_solution(5531090540978855280)
XLA Ops:
  0.6 51.2 %shard_map.68 = (f32[4,16,1024]{2,1,0:T(8,128)}, f32[1,3,16,1024]{3,2,1,0:T(8,128)}) custom-call(f32[4,16,1024]{2,1,0:T(8,128)} %start_ref.1, s32[4,16,1024]{2,1,0:T(8,128)} %soil_ref.1, f32[12]{0:T(128)} %cond_ref.1, f32[12]{0:T(128)} %store_ref.1, f32[3,16,1024]{2,1,0:T(8,128)} %rain_ref.1), custom_call_target="tpu_custom_call" | custom-call | tf_op jit(solution)/shard_map/pallas_call | solution.py:758
  51.9 1.7 %shard_map.69 = (f32[4,16,1024]{2,1,0:T(8,128)}, f32[1,3,16,1024]{3,2,1,0:T(8,128)}) custom-call(f32[4,16,1024]{2,1,0:T(8,128)} %get-tuple-element.4.refs_0_, f32[1,3,16,1024]{3,2,1,0:T(8,128)} %get-tuple-element.5.refs_1_), custom_call_target="tpu_custom_call" | custom-call | tf_op jit(solution)/shard_map/pallas_call | solution.py:809

commit v6 on v5

--- a/solution.py
+++ b/solution.py
@@ -121,8 +121,8 @@
     sec_peers = [lax.rem(sec + k, n_sec) for k in range(1, n_sec)]
     sec_froms = [lax.rem(sec + n_sec - k, n_sec) for k in range(n_sec)]
     gx_peers = [lax.rem(gx + k, n_gx) for k in range(1, n_gx)]
-    swap_size = 2 * rows * (layers * tiles + 1)
-    row_size = 2 * RIM * (layers * tiles + 1)
+    swap_size = rows * (layers * tiles + 1)
+    row_size = RIM * (layers * tiles + 1)
     rain_size = steps * (tiles + 1) * RIM
     land_size = (total // 2) * tiles * RIM
     flow_size = steps * rows * tiles
@@ -132,7 +132,6 @@
         lot = gauge.at[0:size]
         pltpu.make_async_copy(lot, lot, sem).wait()
 
-    parts_of = ((0, ITERS - 1), (ITERS - 1, ITERS))
     everyone = [
         {"sec": mirrored(sec, i, n_sec), "gx": mirrored(gx, j, n_gx)}
         for j in reversed(range(n_gx)) for i in reversed(range(n_sec)) if i + j
@@ -185,6 +184,8 @@
             edge_f[:, rim] = nil(n_sec, RIM, LANES)
             edge_i[:, rim] = nil(n_sec, RIM, LANES, dtype=jnp.int32)
             for c in range(steps - 1):
+                for k in (0, 1):
+                    pack_in[c, k, :, rim] = nil(ITERS, RIM, LANES)
                 for k in range(len(SHIPPED)):
                     landed[c, k, d] = nil(total // 2, tiles, RIM, LANES)
 
@@ -230,31 +231,29 @@
         pl.semaphore_signal(met_sem, inc=1, device_id={"sec": peer}, device_id_type=MESH)
 
     parcels = ((stage_i, soils, edges_i, edge_i), (stage_f, head, edges_f, edge_f))
-    swaps = [[] for _ in range(n_sec)]
+    swaps = []
     for f, (stage, field, edges, edge) in enumerate(parcels):
         for ct in inner:
-            swaps[0].append(pltpu.make_async_copy(
-                stage.at[:, :, lanes_at(here, ct)], field.at[layers_of(sec), ct, own], own_sem
+            swaps.append(pltpu.make_async_copy(
+                stage.at[:, :, lanes_at(here, ct)], field.at[layers_of(sec), ct, own], own_sem.at[f]
             ))
-        swaps[0].append(pltpu.make_async_copy(edges.at[here], edge.at[sec, own], own_sem))
-    for k, peer in enumerate(sec_peers):
-        for f, (stage, field, edges, edge) in enumerate(parcels):
+        swaps.append(pltpu.make_async_copy(edges.at[here], edge.at[sec, own], own_sem.at[f]))
+        for k, peer in enumerate(sec_peers):
             moves = [
                 (stage.at[:, :, lanes_at(place_of(peer), ct)], field.at[layers_of(sec), ct, own]) for ct in inner
             ]
             moves.append((edges.at[place_of(peer)], edge.at[sec, own]))
-            for m, (src, dst) in enumerate(moves):
-                swaps[k + 1].append(pltpu.make_async_remote_copy(
+            for src, dst in moves:
+                swaps.append(pltpu.make_async_remote_copy(
                     src_ref=src,
                     dst_ref=dst,
                     send_sem=swap_send,
-                    recv_sem=swap_recv.at[k],
+                    recv_sem=swap_recv.at[k, f],
                     device_id={"sec": peer},
                     device_id_type=MESH,
                 ))
-    for moves in swaps:
-        for copy in moves:
-            copy.start()
+    for copy in swaps:
+        copy.start()
 
     def toward(d):
         return lax.rem(gx + n_gx - 1, n_gx) if d == 0 else lax.rem(gx + 1, n_gx)
@@ -276,65 +275,98 @@
             device_id_type=MESH,
         )
 
-    def row_copies(k, d):
+    def row_copies(k, f, d):
         src, dst = ends(d)
         s = sec_froms[k]
-        copies = []
-        for f, (_, field, _, edge) in enumerate(parcels):
-            pairs = ((field.at[layers_of(s), 0:tiles, src], field.at[layers_of(s), 0:tiles, dst]),
-                     (edge.at[s, src], edge.at[s, dst]))
-            for m, (a, b) in enumerate(pairs):
-                copies.append(pltpu.make_async_remote_copy(
-                    src_ref=a,
-                    dst_ref=b,
-                    send_sem=row_send.at[d],
-                    recv_sem=row_recv.at[k, d],
-                    device_id={"gx": toward(d)},
-                    device_id_type=MESH,
-                ))
-        return copies
+        _, field, _, edge = parcels[f]
+        pairs = ((field.at[layers_of(s), 0:tiles, src], field.at[layers_of(s), 0:tiles, dst]),
+                 (edge.at[s, src], edge.at[s, dst]))
+        return [
+            pltpu.make_async_remote_copy(
+                src_ref=a,
+                dst_ref=b,
+                send_sem=row_send.at[d],
+                recv_sem=row_recv.at[k, f, d],
+                device_id={"gx": toward(d)},
+                device_id_type=MESH,
+            )
+            for a, b in pairs
+        ]
 
     for d in (0, 1):
         @pl.when(sends_to(d))
         def _(d=d):
             rain_copy(d).start()
 
-    for k in range(n_sec):
-        drain(swap_size, own_sem if k == 0 else swap_recv.at[k - 1])
-        for d in (0, 1):
-            @pl.when(sends_to(d))
-            def _(d=d, k=k):
-                for copy in row_copies(k, d):
-                    copy.start()
-
-    def take_rows(k):
+    def pass_rows(k, f):
+        drain(swap_size, own_sem.at[f] if k == 0 else swap_recv.at[k - 1, f])
         for d in (0, 1):
             @pl.when(sends_to(d))
             def _(d=d):
-                drain(row_size, row_recv.at[k, 1 - d])
-
-    def packed(field, tile, low):
-        outs = nil(ext, LANES)
+                for copy in row_copies(k, f, d):
+                    copy.start()
+
+    def take_rows(k, f):
+        for d in (0, 1):
+            @pl.when(sends_to(d))
+            def _(d=d):
+                drain(row_size, row_recv.at[k, f, 1 - d])
+
+    for k in range(n_sec):
+        pass_rows(k, 0)
+    for k in range(n_sec):
+        pass_rows(k, 1)
+
+    def packed(field, tile, low, at_rows, lane):
+        outs = nil(*lane.shape)
         for l in range(total):
             shift = (RIM * l if low else RIM * l + RIM) % LANES
-            piece = field[1 + l, tile]
+            piece = field[1 + l, tile, at_rows]
             moved = pltpu.roll(piece, shift, 1) if shift else piece
             outs = jnp.where(lane // RIM == l, moved, outs)
         return outs
 
-    def col_copy(c, d, part):
-        low, high = parts_of[part]
+    def beside_to(d):
+        return here > 0 if d == 0 else here < n_sec - 1
+
+    def col_copy(c, d, way):
+        peer = {"sec": place_of(lax.rem(here + n_sec - 1, n_sec) if d == 0 else lax.rem(here + 1, n_sec))}
+        src, dst = (slice(0, rows), own)
+        if way > 0:
+            peer["gx"] = toward(way - 1)
+            src, dst = (slice(0, RIM), slice(ext - RIM, ext)) if way == 1 else (slice(rows - RIM, rows), slice(0, RIM))
         return pltpu.make_async_remote_copy(
-            src_ref=pack_out.at[d, low:high],
-            dst_ref=pack_in.at[c, d, low:high],
-            send_sem=col_send.at[d],
-            recv_sem=col_recv.at[c, d, part],
-            device_id={"sec": place_of(lax.rem(here + n_sec - 1, n_sec) if d == 0 else lax.rem(here + 1, n_sec))},
+            src_ref=pack_out.at[d, :, src],
+            dst_ref=pack_in.at[c, d, :, dst],
+            send_sem=col_send.at[d, way],
+            recv_sem=col_recv.at[c, d, way],
+            device_id=peer,
             device_id_type=MESH,
         )
 
-    def beside_to(d):
-        return here > 0 if d == 0 else here < n_sec - 1
+    def send_cols(c):
+        def each(k, carry):
+            for d in (0, 1):
+                pack_out[d, k] = packed(t.at[k], 0 if d == 0 else tiles - 1, d == 0, own, lane_o)
+            return carry
+
+        lax.fori_loop(0, ITERS, each, 0)
+        for way in (1, 2, 0):
+            for d in (0, 1):
+                @pl.when(beside_to(d) & sends_to(way - 1) if way else beside_to(d))
+                def _(d=d, way=way):
+                    col_copy(c, d, way).start()
+
+    def take_cols(c):
+        for way in (0, 1, 2):
+            for d in (0, 1):
+                @pl.when(beside_to(d) & sends_to(way - 1) if way else beside_to(d))
+                def _(d=d, way=way):
+                    col_copy(c, d, way).wait_send()
+
+                @pl.when(beside_to(d) & sends_to(2 - way) if way else beside_to(d))
+                def _(d=d, way=way):
+                    col_copy(c, 1 - d, way).wait_recv()
 
     def rows_for(k, d, landing):
         if d == 0:
@@ -343,14 +375,14 @@
             start = RIM - LOW + (0 if landing else rows)
         return slice(start, start + k + 1)
 
-    def settle(c, part):
-        low, high = parts_of[part]
-        lots = [p for p, slots in enumerate(SHIPPED) if low <= slots[0][0] < high]
+    def settle(c):
+        lots = range(len(SHIPPED))
         for d in (0, 1):
             @pl.when(sends_to(d))
             def _(d=d):
                 for p in lots:
                     drain(land_size, land_recv.at[c, 1 - d, p])
+                drain(len(SHIPPED) * land_size, land_send.at[d])
 
         def place(i, carry):
             for d in (0, 1):
@@ -364,22 +396,6 @@
             return carry
 
         by_group(0, total // 2, 2, place, 0)
-        for d in (0, 1):
-            @pl.when(beside_to(d))
-            def _(d=d):
-                def each(k, carry):
-                    pack_out[d, k] = packed(t.at[k], 0 if d == 0 else tiles - 1, d == 0)
-                    return carry
-
-                lax.fori_loop(low, high, each, 0)
-                col_copy(c, d, part).start()
-
-    def take_cols(c):
-        for d in (0, 1):
-            @pl.when(beside_to(d))
-            def _(d=d):
-                for part in range(len(parts_of)):
-                    col_copy(c, 1 - d, part).wait_recv()
 
     def side_heads(c, x):
         sides = []
@@ -450,14 +466,14 @@
         of_cond = jnp.where(spot == k, of_kind[0, k], of_cond)
         of_store = jnp.where(spot == k, of_kind[1, k], of_store)
 
-    def open_edges(s):
-        for edge, field in ((edge_f, head), (edge_i, soils)):
-            taken = edge[s]
-            for j in range(layers):
-                moved = pltpu.roll(taken, LANES - RIM - 2 * RIM * j, 1)
-                field[1 + s * layers + j, tiles] = jnp.where(
-                    (lane < RIM) | (lane >= LANES - RIM), moved, nil(ext, LANES, dtype=field.dtype)
-                )
+    def open_edges(s, f):
+        _, field, _, edge = parcels[f]
+        taken = edge[s]
+        for j in range(layers):
+            moved = pltpu.roll(taken, LANES - RIM - 2 * RIM * j, 1)
+            field[1 + s * layers + j, tiles] = jnp.where(
+                (lane < RIM) | (lane >= LANES - RIM), moved, nil(ext, LANES, dtype=field.dtype)
+            )
 
     def look(s):
         for j in range(layers):
@@ -497,11 +513,13 @@
 
         if c == 0:
             for k in range(n_sec):
-                s = sec_froms[k]
-                take_rows(k)
-                open_edges(s)
-                look(s)
-                soil(everywhere, s)
+                take_rows(k, 0)
+                open_edges(sec_froms[k], 0)
+                look(sec_froms[k])
+            for k in range(n_sec):
+                take_rows(k, 1)
+                open_edges(sec_froms[k], 1)
+                soil(everywhere, sec_froms[k])
             for d in (0, 1):
                 @pl.when(sends_to(d))
                 def _(d=d):
@@ -655,27 +673,19 @@
             )
             copy.start()
         if c + 1 < steps:
-            settle(c, 0)
+            send_cols(c)
             if c == 0:
-                side[0] = packed(head, tiles, True)
-                side[1] = packed(head, tiles, False)
-            settle(c, 1)
+                side[0] = packed(head, tiles, True, slice(0, ext), lane)
+                side[1] = packed(head, tiles, False, slice(0, ext), lane)
+            settle(c)
             take_cols(c)
-            for d in (0, 1):
-                @pl.when(sends_to(d))
-                def _(d=d):
-                    drain(len(SHIPPED) * land_size, land_send.at[d])
-
-                @pl.when(beside_to(d))
-                def _(d=d):
-                    drain(ITERS * ext, col_send.at[d])
         drain(len(everyone), sum_recv.at[c])
         drain(len(everyone), sum_send)
         if c == 0:
             for d in (0, 1):
                 @pl.when(sends_to(d))
                 def _(d=d):
-                    drain(n_sec * row_size + rain_size, row_send.at[d])
+                    drain(2 * n_sec * row_size + rain_size, row_send.at[d])
         summed = stats[c, 0]
         for k in range(1, n_sec * n_gx):
             summed = summed + stats[c, k]
@@ -711,7 +721,7 @@
             head.at[layers_of(sec), ct, own], out_ref.at[:, :, lanes_at(here, ct)], out_own
         )
         copy.start()
-    drain((n_sec - 1) * swap_size, swap_send)
+    drain(2 * (n_sec - 1) * swap_size, swap_send)
     drain(flow_size + back_size, out_own)
     drain((n_sec - 1) * (flow_size + back_size), out_send)
     drain((n_sec - 1) * (flow_size + back_size), out_recv)
@@ -770,7 +780,7 @@
         + [
             pltpu.VMEM((steps, tiles + 1, ext, LANES), f32),
             pltpu.VMEM((n_sec, steps, rows, cols), f32),
-            pltpu.VMEM((2, ITERS, ext, LANES), f32),
+            pltpu.VMEM((2, ITERS, rows, LANES), f32),
             pltpu.VMEM((steps - 1, 2, ITERS, ext, LANES), f32),
             pltpu.VMEM((2, ext, LANES), f32),
             pltpu.VMEM((n_sec, ext, LANES), f32),
@@ -788,14 +798,14 @@
             pltpu.SemaphoreType.REGULAR,
             dma,
             dma((2,)),
+            dma((2,)),
             dma,
-            dma,
-            dma((n_sec - 1,)),
+            dma((n_sec - 1, 2)),
             dma((2,)),
-            dma((n_sec, 2)),
+            dma((n_sec, 2, 2)),
             dma((2,)),
-            dma((2,)),
-            dma((steps - 1, 2, 2)),
+            dma((2, 3)),
+            dma((steps - 1, 2, 3)),
             dma((2,)),
             dma((steps - 1, 2, len(SHIPPED))),
             dma,

time: 53.8 us -> 51.6 us (0.959)
  Pallas kernels: 53 us -> 50.8 us
    pallas_call x1, Pallas kernels: 51.2 us -> 49 us  [body(): pl.pallas_call(functools.partial(kernel, n_sec, n_gx, steps, conductivity...]
where the time goes in v6:
time: 51.6 us; the launch traced here: 51.4 us
  Pallas kernels  50.8 us (98%)
  between operations  0.64 us (1%)
    pallas_call x1, Pallas kernels, body(): pl.pallas_call(functools.partial(kernel, n_sec, n_gx, steps, conductivity...  49 us
    pallas_call x1, Pallas kernels, body(): pl.pallas_call(hand_over, out_shape=tuple((jax.ShapeDtypeStruct(a.shape,...  1.75 us

profile of v6, /device:TPU:0, one launch (start us, length us, event | category | flops | bytes accessed | tf_op | source)
XLA Modules:
  0.0 51.4 jit_solution(16408756504730785881)
XLA Ops:
  0.6 49.0 %shard_map.68 = (f32[4,16,1024]{2,1,0:T(8,128)}, f32[1,3,16,1024]{3,2,1,0:T(8,128)}) custom-call(f32[4,16,1024]{2,1,0:T(8,128)} %start_ref.1, s32[4,16,1024]{2,1,0:T(8,128)} %soil_ref.1, f32[12]{0:T(128)} %cond_ref.1, f32[12]{0:T(128)} %store_ref.1, f32[3,16,1024]{2,1,0:T(8,128)} %rain_ref.1), custom_call_target="tpu_custom_call" | custom-call | tf_op jit(solution)/shard_map/pallas_call | solution.py:768
  49.7 1.7 %shard_map.69 = (f32[4,16,1024]{2,1,0:T(8,128)}, f32[1,3,16,1024]{3,2,1,0:T(8,128)}) custom-call(f32[4,16,1024]{2,1,0:T(8,128)} %get-tuple-element.4.refs_0_, f32[1,3,16,1024]{3,2,1,0:T(8,128)} %get-tuple-element.5.refs_1_), custom_call_target="tpu_custom_call" | custom-call | tf_op jit(solution)/shard_map/pallas_call | solution.py:819

commit v7 on v6

--- a/solution.py
+++ b/solution.py
@@ -157,43 +157,6 @@
         return jnp.zeros(shape, dtype)
 
     basis = [t.at[k] for k in range(ITERS)]
-    for ref in (head, cond, face_l, *basis):
-        ref[0] = nil(tiles + 1, ext, LANES)
-        ref[total + 1] = nil(tiles + 1, ext, LANES)
-
-    def hem(l, carry):
-        for ref in (face_r, *basis):
-            ref[l, :, 0:RIM] = nil(tiles + 1, RIM, LANES)
-            ref[l, :, ext - RIM:ext] = nil(tiles + 1, RIM, LANES)
-        return carry
-
-    lax.fori_loop(1, total + 1, hem, 0)
-    for d in (0, 1):
-        rim = slice(ext - RIM, ext) if d == 0 else slice(0, RIM)
-
-        @pl.when(gx == n_gx - 1 if d == 0 else gx == 0)
-        def _(d=d, rim=rim):
-            def wipe(l, carry):
-                head[l + 1, :, rim] = nil(tiles + 1, RIM, LANES)
-                soils[l + 1, :, rim] = nil(tiles + 1, RIM, LANES, dtype=jnp.int32)
-                return carry
-
-            lax.fori_loop(0, total, wipe, 0)
-            for c in range(steps):
-                rainx[c, :, rim] = nil(tiles + 1, RIM, LANES)
-            edge_f[:, rim] = nil(n_sec, RIM, LANES)
-            edge_i[:, rim] = nil(n_sec, RIM, LANES, dtype=jnp.int32)
-            for c in range(steps - 1):
-                for k in (0, 1):
-                    pack_in[c, k, :, rim] = nil(ITERS, RIM, LANES)
-                for k in range(len(SHIPPED)):
-                    landed[c, k, d] = nil(total // 2, tiles, RIM, LANES)
-
-        @pl.when(here == n_sec - 1 if d == 0 else here == 0)
-        def _(d=d):
-            for c in range(steps - 1):
-                pack_in[c, d] = nil(ITERS, ext, LANES)
-
     lane = lax.broadcasted_iota(jnp.int32, (ext, LANES), 1)
     lane_w = lax.broadcasted_iota(jnp.int32, (rows + RIM, LANES), 1)
     lane_o = lax.broadcasted_iota(jnp.int32, (rows, LANES), 1)
@@ -205,12 +168,6 @@
 
     drain((2 * layers + steps) * rows * wide // LANES, load_sem)
 
-    after = lanes_at(lax.rem(here + 1, n_sec), 0)
-    before = lanes_at(lax.rem(here + n_sec - 1, n_sec), tiles - 1)
-    for c in range(steps):
-        for ct in inner:
-            rainx[c, ct, own] = stage_r[c, :, lanes_at(here, ct)]
-        rainx[c, tiles, own] = jnp.where(lane_o < LANES // 2, stage_r[c, :, after], stage_r[c, :, before])
     for stage, edges in ((stage_f, edges_f), (stage_i, edges_i)):
         for place in range(n_sec):
             out = nil(rows, LANES, dtype=stage.dtype)
@@ -255,6 +212,49 @@
     for copy in swaps:
         copy.start()
 
+    for ref in (head, cond, face_l, *basis):
+        ref[0] = nil(tiles + 1, ext, LANES)
+        ref[total + 1] = nil(tiles + 1, ext, LANES)
+
+    def hem(l, carry):
+        for ref in (face_r, *basis):
+            ref[l, :, 0:RIM] = nil(tiles + 1, RIM, LANES)
+            ref[l, :, ext - RIM:ext] = nil(tiles + 1, RIM, LANES)
+        return carry
+
+    lax.fori_loop(1, total + 1, hem, 0)
+    for d in (0, 1):
+        rim = slice(ext - RIM, ext) if d == 0 else slice(0, RIM)
+
+        @pl.when(gx == n_gx - 1 if d == 0 else gx == 0)
+        def _(d=d, rim=rim):
+            def wipe(l, carry):
+                head[l + 1, :, rim] = nil(tiles + 1, RIM, LANES)
+                soils[l + 1, :, rim] = nil(tiles + 1, RIM, LANES, dtype=jnp.int32)
+                return carry
+
+            lax.fori_loop(0, total, wipe, 0)
+            for c in range(steps):
+                rainx[c, :, rim] = nil(tiles + 1, RIM, LANES)
+            edge_f[:, rim] = nil(n_sec, RIM, LANES)
+            edge_i[:, rim] = nil(n_sec, RIM, LANES, dtype=jnp.int32)
+            for c in range(steps - 1):
+                for k in (0, 1):
+                    pack_in[c, k, :, rim] = nil(ITERS, RIM, LANES)
+                for k in range(len(SHIPPED)):
+                    landed[c, k, d] = nil(total // 2, tiles, RIM, LANES)
+
+        @pl.when(here == n_sec - 1 if d == 0 else here == 0)
+        def _(d=d):
+            for c in range(steps - 1):
+                pack_in[c, d] = nil(ITERS, ext, LANES)
+
+    after = lanes_at(lax.rem(here + 1, n_sec), 0)
+    before = lanes_at(lax.rem(here + n_sec - 1, n_sec), tiles - 1)
+    for c in range(steps):
+        for ct in inner:
+            rainx[c, ct, own] = stage_r[c, :, lanes_at(here, ct)]
+        rainx[c, tiles, own] = jnp.where(lane_o < LANES // 2, stage_r[c, :, after], stage_r[c, :, before])
     def toward(d):
         return lax.rem(gx + n_gx - 1, n_gx) if d == 0 else lax.rem(gx + 1, n_gx)
 
@@ -613,8 +613,8 @@
         for k in range(ITERS - 1):
             def apply(i, acc, k=k):
                 v_of = basis[k]
-                for j in range(layers):
-                    l = 1 + i * layers + j
+                for j in range(2 * layers):
+                    l = 1 + i * 2 * layers + j
                     v = [v_of[l, ct, work] for ct in everywhere]
                     fc = [face_c[l, ct, work] for ct in everywhere]
                     aside = right_of(v, lane_w)
@@ -628,11 +628,11 @@
                         basis[k + 1][l, ct, work] = new
                         if ct < tiles:
                             acc = (acc[0] + own_of(v[ct] * near), acc[1] + own_of(diag[l, ct, work] * new * new))
-                for j in range(0, layers, 2):
-                    rows_of(k + 1, 1 + i * layers + j)
+                for j in range(0, 2 * layers, 2):
+                    rows_of(k + 1, 1 + i * 2 * layers + j)
                 return acc
 
-            ah, ag = lax.fori_loop(0, n_sec, apply, (none, none))
+            ah, ag = lax.fori_loop(0, n_sec // 2, apply, (none, none))
             h.append(ah)
             g.append(ag)
             send_land(k + 1)

time: 51.6 us -> 50.8 us (0.984)
  Pallas kernels: 50.8 us -> 50 us
    pallas_call x1, Pallas kernels: 49 us -> 48.3 us  [body(): pl.pallas_call(functools.partial(kernel, n_sec, n_gx, steps, conductivity...]
where the time goes in v7:
time: 50.8 us; the launch traced here: 50.7 us
  Pallas kernels  50 us (98%)
  between operations  0.64 us (1%)
    pallas_call x1, Pallas kernels, body(): pl.pallas_call(functools.partial(kernel, n_sec, n_gx, steps, conductivity...  48.3 us
    pallas_call x1, Pallas kernels, body(): pl.pallas_call(hand_over, out_shape=tuple((jax.ShapeDtypeStruct(a.shape,...  1.75 us

profile of v7, /device:TPU:0, one launch (start us, length us, event | category | flops | bytes accessed | tf_op | source)
XLA Modules:
  0.0 50.7 jit_solution(5660678132396346675)
XLA Ops:
  0.6 48.3 %shard_map.68 = (f32[4,16,1024]{2,1,0:T(8,128)}, f32[1,3,16,1024]{3,2,1,0:T(8,128)}) custom-call(f32[4,16,1024]{2,1,0:T(8,128)} %start_ref.1, s32[4,16,1024]{2,1,0:T(8,128)} %soil_ref.1, f32[12]{0:T(128)} %cond_ref.1, f32[12]{0:T(128)} %store_ref.1, f32[3,16,1024]{2,1,0:T(8,128)} %rain_ref.1), custom_call_target="tpu_custom_call" | custom-call | tf_op jit(solution)/shard_map/pallas_call | solution.py:768
  48.9 1.7 %shard_map.69 = (f32[4,16,1024]{2,1,0:T(8,128)}, f32[1,3,16,1024]{3,2,1,0:T(8,128)}) custom-call(f32[4,16,1024]{2,1,0:T(8,128)} %get-tuple-element.4.refs_0_, f32[1,3,16,1024]{3,2,1,0:T(8,128)} %get-tuple-element.5.refs_1_), custom_call_target="tpu_custom_call" | custom-call | tf_op jit(solution)/shard_map/pallas_call | solution.py:819

commit v8 on v7

--- a/solution.py
+++ b/solution.py
@@ -546,7 +546,7 @@
             )
             copy.start()
 
-        by_group(1, total + 1, layers, faces, 0)
+        by_group(1, total + 1, 2 * layers, faces, 0)
 
         def rows_of(k, l):
             if c + 1 < steps:
@@ -648,7 +648,7 @@
                     acc = acc + near[i:i + RIM]
             return acc
 
-        h.append(2.0 * by_group(1, total + 1, layers, last, none))
+        h.append(2.0 * by_group(1, total + 1, 2 * layers, last, none))
 
         flat = jnp.concatenate([jnp.sum(v, axis=0, keepdims=True) for v in g + h], axis=0)
         part = LANES // (2 * ITERS)
@@ -713,7 +713,7 @@
                     copy.start()
             by_group(1 + sec * layers, 1 + (sec + 1) * layers, layers, final, 0)
         else:
-            by_group(1, total + 1, layers, functools.partial(update, inner, slice(0, ext), ext), 0)
+            by_group(1, total + 1, 2 * layers, functools.partial(update, inner, slice(0, ext), ext), 0)
             side_heads(c, x)
 
     for ct in inner:

time: 50.8 us -> 50.2 us (0.988)
  Pallas kernels: 50 us -> 49.4 us
    pallas_call x1, Pallas kernels: 48.3 us -> 47.7 us  [body(): pl.pallas_call(functools.partial(kernel, n_sec, n_gx, steps, conductivity...]
where the time goes in v8:
time: 50.2 us; the launch traced here: 50.1 us
  Pallas kernels  49.4 us (98%)
  between operations  0.64 us (1%)
    pallas_call x1, Pallas kernels, body(): pl.pallas_call(functools.partial(kernel, n_sec, n_gx, steps, conductivity...  47.7 us
    pallas_call x1, Pallas kernels, body(): pl.pallas_call(hand_over, out_shape=tuple((jax.ShapeDtypeStruct(a.shape,...  1.75 us

profile of v8, /device:TPU:0, one launch (start us, length us, event | category | flops | bytes accessed | tf_op | source)
XLA Modules:
  0.0 50.1 jit_solution(17835577126483159936)
XLA Ops:
  0.6 47.7 %shard_map.68 = (f32[4,16,1024]{2,1,0:T(8,128)}, f32[1,3,16,1024]{3,2,1,0:T(8,128)}) custom-call(f32[4,16,1024]{2,1,0:T(8,128)} %start_ref.1, s32[4,16,1024]{2,1,0:T(8,128)} %soil_ref.1, f32[12]{0:T(128)} %cond_ref.1, f32[12]{0:T(128)} %store_ref.1, f32[3,16,1024]{2,1,0:T(8,128)} %rain_ref.1), custom_call_target="tpu_custom_call" | custom-call | tf_op jit(solution)/shard_map/pallas_call | solution.py:768
  48.3 1.7 %shard_map.69 = (f32[4,16,1024]{2,1,0:T(8,128)}, f32[1,3,16,1024]{3,2,1,0:T(8,128)}) custom-call(f32[4,16,1024]{2,1,0:T(8,128)} %get-tuple-element.4.refs_0_, f32[1,3,16,1024]{3,2,1,0:T(8,128)} %get-tuple-element.5.refs_1_), custom_call_target="tpu_custom_call" | custom-call | tf_op jit(solution)/shard_map/pallas_call | solution.py:819
